TPU v7x, 256 devices: a whole 4x4x8 slice. The times are simulated.
256 devices in a mesh: seq: 128 (over y, z, x), head: 2 (over core).
Axes of the slice: x: 4, y: 4, z: 8, core: 2. Of those that a mesh axis runs over, the one named last changes fastest.
Arguments:
- tokens: bfloat16 [1024, 64, 2048], P('seq'), may hold values from -64 to 64
- w_qkv: bfloat16 [3, 2048, 1024], P(None, None, 'head'), may hold values from -1 to 1
- conv_taps: float32 [3, 3, 1024], P(None, None, 'head'), may hold values from -1 to 1
- w_out: bfloat16 [1024, 2048], P('head'), may hold values from -0.1875 to 0.1875
- episode_start: int32 [1024], P('seq'), may hold values from 0 to 1023, as said below
Outputs:
- sublayer_out: bfloat16 [1024, 64, 2048], P('seq', None, 'head')
Inputs may be any that keep to these rules, and one draw needn't show every extreme that they name: episode_start[t] is the first frame of the episode holding frame t; episodes are runs of 1 to 64 consecutive frames, and one has exactly 64.
All inputs are finite; a program needn't handle non-finite values.
Results may differ from a plain program's by a relative error of at most 0.006.
The roundings to bfloat16 on the way count: a program that leaves them out, or rounds other values in their place, can miss the bound.
Values may be sent and summed in bfloat16 or wider, within the bound.
No kernel may reach another device: no remote copies, remote signals or barrier semaphores. Data moves between devices by JAX's collectives and lax.ppermute only.
A program may use at most 128 MiB of HBM per device.

v0:
```python
import math

import jax
import jax.numpy as jnp
from jax import lax
from jax.sharding import PartitionSpec as P

HEAD_DIM = 128
REACH = 8


def shifted_2(value, axis, steps):
    count = lax.axis_size(axis)
    first, last = (max(0, -steps), min(count, count - steps))
    return lax.ppermute(value, axis, [(source, source + steps) for source in range(first, last)])


def attend(queries, keys_in, values_in, starts, first_query, first_key, head_dim):
    query_len, positions, inner_width = queries.shape
    key_len = keys_in.shape[0]
    head_count = inner_width // head_dim
    query_heads = queries.reshape(query_len, positions, head_count, head_dim)
    key_heads = keys_in.reshape(key_len, positions, head_count, head_dim)
    value_heads = values_in.reshape(key_len, positions, head_count, head_dim)
    scores = jnp.einsum(
        "qphd,kphd->phqk", query_heads, key_heads, preferred_element_type=jnp.float32
    ) / math.sqrt(head_dim)
    qframe = first_query + jnp.arange(query_len, dtype=jnp.int32)
    kframe = first_key + jnp.arange(key_len, dtype=jnp.int32)
    allowed = (kframe[None, :] >= starts[:, None]) & (kframe[None, :] <= qframe[:, None])
    masked = jnp.where(allowed[None, None], scores, -1e30)
    row_max = jnp.max(masked, axis=-1, keepdims=True)
    unnorm = jnp.where(allowed[None, None], jnp.exp(masked - row_max), 0.0)
    probs = (unnorm / jnp.sum(unnorm, axis=-1, keepdims=True)).astype(jnp.bfloat16)
    result = jnp.einsum("phqk,kphd->qphd", probs, value_heads, preferred_element_type=jnp.float32)
    return result.reshape(query_len, positions, inner_width).astype(jnp.bfloat16)


def shards(tokens, w_qkv, conv_taps, w_out, episode_start):
    frames, positions, model_width = tokens.shape
    inner_width = w_qkv.shape[2]
    seq_index = lax.axis_index("seq")
    first_frame = seq_index * frames
    tokens_f = tokens.astype(jnp.float32)
    inv_rms = lax.rsqrt(jnp.mean(tokens_f * tokens_f, axis=-1, keepdims=True) + 1e-06)
    normed = (tokens_f * inv_rms).astype(jnp.bfloat16)
    projected = jnp.einsum(
        "nd,cde->cne",
        normed.reshape(frames * positions, model_width),
        w_qkv,
        preferred_element_type=jnp.float32,
    ).reshape(3, frames, positions, inner_width)
    before = shifted_2(projected[:, frames - 2 :], "seq", 1)
    padded = jnp.concatenate([before, projected], axis=1)
    frame_ids = first_frame + jnp.arange(frames, dtype=jnp.int32)
    convolved = jnp.zeros_like(projected)
    for frame_lag in range(3):
        shifted = padded[:, 2 - frame_lag : 2 - frame_lag + frames]
        in_episode = (frame_ids - frame_lag >= episode_start).astype(jnp.float32)
        convolved = (
            convolved
            + conv_taps[frame_lag][:, None, None, :] * shifted * in_episode[None, :, None, None]
        )
    convolved = convolved.astype(jnp.bfloat16)
    key_value = convolved[1:]
    blocks = [key_value]
    moving = key_value
    for distance in range(REACH):
        moving = shifted_2(moving, "seq", 1)
        blocks.append(moving)
    window = jnp.concatenate(blocks[::-1], axis=1)
    attended = attend(
        convolved[0],
        window[0],
        window[1],
        episode_start,
        first_frame,
        first_frame - REACH * frames,
        HEAD_DIM,
    )
    partial_value = jnp.dot(
        attended.reshape(frames * positions, inner_width), w_out, preferred_element_type=jnp.float32
    )
    partial_value = partial_value.reshape(frames, positions, model_width)
    return lax.psum_scatter(partial_value, "head", scatter_dimension=2, tiled=True).astype(
        jnp.bfloat16
    )


def solution(mesh):
    in_specs = (
        P("seq", None, None),
        P(None, None, "head"),
        P(None, None, "head"),
        P("head", None),
        P("seq"),
    )
    out_specs = P("seq", None, "head")
    return jax.shard_map(shards, mesh=mesh, in_specs=in_specs, out_specs=out_specs, check_vma=False)
```

profile of v0, /device:TPU:1, one launch (start us, length us, event | category | flops | bytes accessed | tf_op | source)
XLA Modules:
  0.0 352.3 jit_solution(15598257760684839209)
XLA Ops:
  6.5 2.2 fusion.5
  8.8 2.4 fusion.6
  11.2 3.4 fusion.40
  14.6 1.6 copy-done.3
  17.2 4.0 %collective-permute-start = (f32[3,2,64,512]{3,2,1,0:T(8,128)}, f32[3,2,64,512]{3,2,1,0:T(8,128)S(1)}, u32[]{:S(2)}, u32[]{:S(2)}) collective-permute-start(f32[3,2,64,512]{3,2,1,0:T(8,128)} %slice.40), channel_id=1, source_target_pairs={{0,2},{2,4},{4,6},{6,8},{8,10},{10,12},{12,14},{14,16},{16,18},{18... | collective-permute-start | bytes 2359304 | tf_op jit(solution)/shard_map/ppermute | solution.py:15
  21.2 16.4 %collective-permute-done = f32[3,2,64,512]{3,2,1,0:T(8,128)S(1)} collective-permute-done((f32[3,2,64,512]{3,2,1,0:T(8,128)}, f32[3,2,64,512]{3,2,1,0:T(8,128)S(1)}, u32[]{:S(2)}, u32[]{:S(2)}) %collective-permute-start) | collective-permute-done | bytes 786464 | tf_op jit(solution)/shard_map/ppermute | solution.py:15
  37.6 4.3 %fusion.12 = bf16[3,8,64,512]{3,2,1,0:T(8,128)(2,1)S(1)} fusion(f32[3,2,64,512]{3,2,1,0:T(8,128)S(1)} %collective-permute-done, f32[3,8,64,512]{3,2,1,0:T(8,128)} %bitcast.27, f32[8]{0:T(128)S(1)} %get-tuple-element.12, f32[3,512]{1,0:T(4,128)S(1)} %get-tuple-element.8, f32[8]{0:T(128)S(1)} %get-tuple-element.11, f32[3,512]{1,0:T(4,128)S(1)} %get-tuple-element.9, ...), kind=kLoop, calls=%fused_computation.16 | loop fusion | flops 8650752 | bytes 5523552 | tf_op jit(solution)/shard_map/convert_element_type | solution.py:64
  42.0 1.1 copy-done.1
  43.2 4.1 %collective-permute-start.1 = (bf16[2,8,64,512]{3,2,1,0:T(8,128)(2,1)S(1)}, bf16[2,8,64,512]{3,2,1,0:T(8,128)(2,1)S(1)}, u32[]{:S(2)}, u32[]{:S(2)}) collective-permute-start(bf16[2,8,64,512]{3,2,1,0:T(8,128)(2,1)S(1)} %slice.43), channel_id=1, source_target_pairs={{0,2},{2,4},{4,6},{6,8},{8,10},{10,12},{12,14},{14,16},{16,18},{18... | collective-permute-start | bytes 3145736 | tf_op jit(solution)/shard_map/ppermute | solution.py:15
  47.2 20.9 %collective-permute-done.1 = bf16[2,8,64,512]{3,2,1,0:T(8,128)(2,1)S(1)} collective-permute-done((bf16[2,8,64,512]{3,2,1,0:T(8,128)(2,1)S(1)}, bf16[2,8,64,512]{3,2,1,0:T(8,128)(2,1)S(1)}, u32[]{:S(2)}, u32[]{:S(2)}) %collective-permute-start.1) | collective-permute-done | bytes 1048608 | tf_op jit(solution)/shard_map/ppermute | solution.py:15
  68.1 1.0 copy-done.4
  69.1 4.2 %collective-permute-start.2 = (bf16[2,8,64,512]{3,2,1,0:T(8,128)(2,1)S(1)}, bf16[2,8,64,512]{3,2,1,0:T(8,128)(2,1)S(1)}, u32[]{:S(2)}, u32[]{:S(2)}) collective-permute-start(bf16[2,8,64,512]{3,2,1,0:T(8,128)(2,1)S(1)} %collective-permute-done.1), channel_id=1, source_target_pairs={{0,2},{2,4},{4,6},{6,8},{8,10},{10,12},{12,14},{14,16},{16,18},{18... | collective-permute-start | bytes 3145736 | tf_op jit(solution)/shard_map/ppermute | solution.py:15
  73.3 20.0 %collective-permute-done.2 = bf16[2,8,64,512]{3,2,1,0:T(8,128)(2,1)S(1)} collective-permute-done((bf16[2,8,64,512]{3,2,1,0:T(8,128)(2,1)S(1)}, bf16[2,8,64,512]{3,2,1,0:T(8,128)(2,1)S(1)}, u32[]{:S(2)}, u32[]{:S(2)}) %collective-permute-start.2) | collective-permute-done | bytes 1048608 | tf_op jit(solution)/shard_map/ppermute | solution.py:15
  93.3 1.0 copy-done.6
  94.3 4.2 %collective-permute-start.3 = (bf16[2,8,64,512]{3,2,1,0:T(8,128)(2,1)S(1)}, bf16[2,8,64,512]{3,2,1,0:T(8,128)(2,1)S(1)}, u32[]{:S(2)}, u32[]{:S(2)}) collective-permute-start(bf16[2,8,64,512]{3,2,1,0:T(8,128)(2,1)S(1)} %collective-permute-done.2), channel_id=1, source_target_pairs={{0,2},{2,4},{4,6},{6,8},{8,10},{10,12},{12,14},{14,16},{16,18},{18... | collective-permute-start | bytes 3145736 | tf_op jit(solution)/shard_map/ppermute | solution.py:15
  98.5 19.2 %collective-permute-done.3 = bf16[2,8,64,512]{3,2,1,0:T(8,128)(2,1)S(1)} collective-permute-done((bf16[2,8,64,512]{3,2,1,0:T(8,128)(2,1)S(1)}, bf16[2,8,64,512]{3,2,1,0:T(8,128)(2,1)S(1)}, u32[]{:S(2)}, u32[]{:S(2)}) %collective-permute-start.3) | collective-permute-done | bytes 1048608 | tf_op jit(solution)/shard_map/ppermute | solution.py:15
  117.7 1.0 copy-done.8
  118.7 4.2 %collective-permute-start.4 = (bf16[2,8,64,512]{3,2,1,0:T(8,128)(2,1)S(1)}, bf16[2,8,64,512]{3,2,1,0:T(8,128)(2,1)S(1)}, u32[]{:S(2)}, u32[]{:S(2)}) collective-permute-start(bf16[2,8,64,512]{3,2,1,0:T(8,128)(2,1)S(1)} %collective-permute-done.3), channel_id=1, source_target_pairs={{0,2},{2,4},{4,6},{6,8},{8,10},{10,12},{12,14},{14,16},{16,18},{18... | collective-permute-start | bytes 3145736 | tf_op jit(solution)/shard_map/ppermute | solution.py:15
  122.8 18.3 %collective-permute-done.4 = bf16[2,8,64,512]{3,2,1,0:T(8,128)(2,1)S(1)} collective-permute-done((bf16[2,8,64,512]{3,2,1,0:T(8,128)(2,1)S(1)}, bf16[2,8,64,512]{3,2,1,0:T(8,128)(2,1)S(1)}, u32[]{:S(2)}, u32[]{:S(2)}) %collective-permute-start.4) | collective-permute-done | bytes 1048608 | tf_op jit(solution)/shard_map/ppermute | solution.py:15
  141.2 1.0 copy-done.10
  142.1 5.5 %collective-permute-start.5 = (bf16[2,8,64,512]{3,2,1,0:T(8,128)(2,1)S(1)}, bf16[2,8,64,512]{3,2,1,0:T(8,128)(2,1)S(1)}, u32[]{:S(2)}, u32[]{:S(2)}) collective-permute-start(bf16[2,8,64,512]{3,2,1,0:T(8,128)(2,1)S(1)} %collective-permute-done.4), channel_id=1, source_target_pairs={{0,2},{2,4},{4,6},{6,8},{8,10},{10,12},{12,14},{14,16},{16,18},{18... | collective-permute-start | bytes 3145736 | tf_op jit(solution)/shard_map/ppermute | solution.py:15
  147.6 17.5 %collective-permute-done.5 = bf16[2,8,64,512]{3,2,1,0:T(8,128)(2,1)S(1)} collective-permute-done((bf16[2,8,64,512]{3,2,1,0:T(8,128)(2,1)S(1)}, bf16[2,8,64,512]{3,2,1,0:T(8,128)(2,1)S(1)}, u32[]{:S(2)}, u32[]{:S(2)}) %collective-permute-start.5) | collective-permute-done | bytes 1048608 | tf_op jit(solution)/shard_map/ppermute | solution.py:15
  165.1 1.0 copy-done.12
  166.1 6.3 %collective-permute-start.6 = (bf16[2,8,64,512]{3,2,1,0:T(8,128)(2,1)S(1)}, bf16[2,8,64,512]{3,2,1,0:T(8,128)(2,1)S(1)}, u32[]{:S(2)}, u32[]{:S(2)}) collective-permute-start(bf16[2,8,64,512]{3,2,1,0:T(8,128)(2,1)S(1)} %collective-permute-done.5), channel_id=1, source_target_pairs={{0,2},{2,4},{4,6},{6,8},{8,10},{10,12},{12,14},{14,16},{16,18},{18... | collective-permute-start | bytes 3145736 | tf_op jit(solution)/shard_map/ppermute | solution.py:15
  172.4 16.6 %collective-permute-done.6 = bf16[2,8,64,512]{3,2,1,0:T(8,128)(2,1)S(1)} collective-permute-done((bf16[2,8,64,512]{3,2,1,0:T(8,128)(2,1)S(1)}, bf16[2,8,64,512]{3,2,1,0:T(8,128)(2,1)S(1)}, u32[]{:S(2)}, u32[]{:S(2)}) %collective-permute-start.6) | collective-permute-done | bytes 1048608 | tf_op jit(solution)/shard_map/ppermute | solution.py:15
  189.0 1.0 copy-done.14
  190.0 7.2 %collective-permute-start.7 = (bf16[2,8,64,512]{3,2,1,0:T(8,128)(2,1)S(1)}, bf16[2,8,64,512]{3,2,1,0:T(8,128)(2,1)}, u32[]{:S(2)}, u32[]{:S(2)}) collective-permute-start(bf16[2,8,64,512]{3,2,1,0:T(8,128)(2,1)S(1)} %collective-permute-done.6), channel_id=1, source_target_pairs={{0,2},{2,4},{4,6},{6,8},{8,10},{10,12},{12,14},{14,16},{16,18},{18... | collective-permute-start | bytes 3145736 | tf_op jit(solution)/shard_map/ppermute | solution.py:15
  197.2 14.9 %collective-permute-done.7 = bf16[2,8,64,512]{3,2,1,0:T(8,128)(2,1)} collective-permute-done((bf16[2,8,64,512]{3,2,1,0:T(8,128)(2,1)S(1)}, bf16[2,8,64,512]{3,2,1,0:T(8,128)(2,1)}, u32[]{:S(2)}, u32[]{:S(2)}) %collective-permute-start.7) | collective-permute-done | bytes 1048608 | tf_op jit(solution)/shard_map/ppermute | solution.py:15
  212.0 7.2 %collective-permute-start.8 = (bf16[2,8,64,512]{3,2,1,0:T(8,128)(2,1)}, bf16[2,8,64,512]{3,2,1,0:T(8,128)(2,1)}, u32[]{:S(2)}, u32[]{:S(2)}) collective-permute-start(bf16[2,8,64,512]{3,2,1,0:T(8,128)(2,1)} %collective-permute-done.7), channel_id=1, source_target_pairs={{0,2},{2,4},{4,6},{6,8},{8,10},{10,12},{12,14},{14,16},{16,18},{18... | collective-permute-start | bytes 3145736 | tf_op jit(solution)/shard_map/ppermute | solution.py:15
  219.3 1.1 slice.45
  220.6 13.2 %collective-permute-done.8 = bf16[2,8,64,512]{3,2,1,0:T(8,128)(2,1)} collective-permute-done((bf16[2,8,64,512]{3,2,1,0:T(8,128)(2,1)}, bf16[2,8,64,512]{3,2,1,0:T(8,128)(2,1)}, u32[]{:S(2)}, u32[]{:S(2)}) %collective-permute-start.8) | collective-permute-done | bytes 1048608 | tf_op jit(solution)/shard_map/ppermute | solution.py:15
  233.7 2.3 constant_dynamic-update-slice_fusion.8
  236.0 2.4 constant_dynamic-update-slice_fusion.7
  238.4 1.1 constant_dynamic-update-slice_fusion.6
  239.5 1.1 constant_dynamic-update-slice_fusion.5
  240.6 1.1 constant_dynamic-update-slice_fusion.4
  241.7 1.1 constant_dynamic-update-slice_fusion.3
  242.8 1.1 constant_dynamic-update-slice_fusion.2
  243.9 1.1 constant_dynamic-update-slice_fusion.1
  245.0 1.1 constant_dynamic-update-slice_fusion
  246.1 8.9 %fusion.34 = (bf16[1,72,64,512]{3,2,1,0:T(8,128)(2,1)}, bf16[1,72,64,512]{3,2,1,0:T(8,128)(2,1)}) fusion(bf16[2,72,64,512]{3,2,1,0:T(8,128)(2,1)} %constant_dynamic-update-slice_fusion), kind=kLoop, calls=%fused_computation.51 | loop fusion | bytes 18874368 | tf_op jit(solution)/shard_map/slice | solution.py:74
  254.9 7.7 %reshape_squeeze.11 = bf16[72,64,4,128]{3,2,1,0:T(4,128)(2,1)} reshape(bf16[1,72,64,512]{3,2,1,0:T(8,128)(2,1)} %get-tuple-element.5) | data formatting | bytes 9437184 | tf_op jit(solution)/shard_map/reshape;squeeze | solution.py:23
  262.6 7.7 %reshape_squeeze.9 = bf16[72,64,4,128]{3,2,1,0:T(4,128)(2,1)} reshape(bf16[1,72,64,512]{3,2,1,0:T(8,128)(2,1)} %get-tuple-element.6) | data formatting | bytes 9437184 | tf_op jit(solution)/shard_map/reshape;squeeze | solution.py:24
  270.3 7.4 %fusion.35 = (f32[64,4,8]{2,1,0:T(4,128)S(1)}, f32[64,4,8,72]{3,2,1,0:T(8,128)}) fusion(pred[8,72]{1,0:T(8,128)(4,1)S(1)} %compare_and_fusion, bf16[72,64,4,128]{3,2,1,0:T(4,128)(2,1)} %reshape_squeeze.11, bf16[8,64,4,128]{3,2,1,0:T(4,128)(2,1)S(1)} %reshape_squeeze.10), kind=kOutput, calls=%fused_computation.52 | convolution fusion | flops 38486088 | bytes 5841472 | tf_op jit(solution)/shard_map/sub | solution.py:33
  277.7 6.0 %fusion.29 = bf16[8,64,4,128]{3,0,2,1:T(8,128)(2,1)S(1)} fusion(bf16[72,64,4,128]{3,2,1,0:T(4,128)(2,1)} %reshape_squeeze.9, f32[64,4,8,72]{3,2,1,0:T(8,128)} %get-tuple-element.14, f32[64,4,8]{2,1,0:T(4,128)S(1)} %get-tuple-element.13), kind=kOutput, calls=%fused_computation.28 | convolution fusion | flops 38305792 | bytes 5840896 | tf_op jit(solution)/shard_map/phqk,kphd->qphd/dot_general | solution.py:35
  284.2 3.2 fusion.15
  287.4 55.3 %reduce-scatter.2.cloned.1.call-done = f32[8,64,1024]{2,1,0:T(8,128)} async-done(((f32[8,64,2048]{2,1,0:T(8,128)}), f32[8,64,1024]{2,1,0:T(8,128)}) %reduce-scatter.2.cloned.1.call-update) | async-done | bytes 2097168 | tf_op jit(solution)/shard_map/reduce_scatter | solution.py:85
  342.7 2.7 convert_element_type.45
  (43 shorter events, 1.7 us)
Async XLA Ops:
  6.5 277.6 %copy-start = (bf16[512,2048]{1,0:T(8,128)(2,1)S(1)}, bf16[512,2048]{1,0:T(8,128)(2,1)}, u32[]{:S(2)}) copy-start(bf16[512,2048]{1,0:T(8,128)(2,1)} %param.8) | copy-start | bytes 6291460
  6.5 336.2 %reduce-scatter.2.cloned.1.call-start = ((), (), s32[]{:S(2)}) async-start(), calls=%async_computation.1 | async-start | bytes 6291456 | tf_op jit(solution)/shard_map/reduce_scatter | solution.py:85
  6.5 4.6 %copy-start.18 = (bf16[3,2048,512]{2,1,0:T(8,128)(2,1)S(1)}, bf16[3,2048,512]{2,1,0:T(8,128)(2,1)}, u32[]{:S(2)}) copy-start(bf16[3,2048,512]{2,1,0:T(8,128)(2,1)} %param.6) | copy-start | bytes 18874372
  11.1 10.0 %copy-start.17 = (s32[8]{0:T(128)S(1)}, s32[8]{0:T(128)}, u32[]{:S(2)}) copy-start(s32[8]{0:T(128)} %param.9) | copy-start | bytes 100
  11.2 10.0 %copy-start.16 = (f32[3,3,512]{2,1,0:T(4,128)S(1)}, f32[3,3,512]{2,1,0:T(4,128)}, u32[]{:S(2)}) copy-start(f32[3,3,512]{2,1,0:T(4,128)} %param.7) | copy-start | bytes 55300
  14.6 1.6 copy-start.3
  17.2 20.4 %collective-permute-start = (f32[3,2,64,512]{3,2,1,0:T(8,128)}, f32[3,2,64,512]{3,2,1,0:T(8,128)S(1)}, u32[]{:S(2)}, u32[]{:S(2)}) collective-permute-start(f32[3,2,64,512]{3,2,1,0:T(8,128)} %slice.40), channel_id=1, source_target_pairs={{0,2},{2,4},{4,6},{6,8},{8,10},{10,12},{12,14},{14,16},{16,18},{18... | collective-permute-start | bytes 2359304 | tf_op jit(solution)/shard_map/ppermute | solution.py:15
  42.0 1.1 copy-start.1
  43.2 25.0 %collective-permute-start.1 = (bf16[2,8,64,512]{3,2,1,0:T(8,128)(2,1)S(1)}, bf16[2,8,64,512]{3,2,1,0:T(8,128)(2,1)S(1)}, u32[]{:S(2)}, u32[]{:S(2)}) collective-permute-start(bf16[2,8,64,512]{3,2,1,0:T(8,128)(2,1)S(1)} %slice.43), channel_id=1, source_target_pairs={{0,2},{2,4},{4,6},{6,8},{8,10},{10,12},{12,14},{14,16},{16,18},{18... | collective-permute-start | bytes 3145736 | tf_op jit(solution)/shard_map/ppermute | solution.py:15
  68.1 1.0 copy-start.4
  69.1 24.2 %collective-permute-start.2 = (bf16[2,8,64,512]{3,2,1,0:T(8,128)(2,1)S(1)}, bf16[2,8,64,512]{3,2,1,0:T(8,128)(2,1)S(1)}, u32[]{:S(2)}, u32[]{:S(2)}) collective-permute-start(bf16[2,8,64,512]{3,2,1,0:T(8,128)(2,1)S(1)} %collective-permute-done.1), channel_id=1, source_target_pairs={{0,2},{2,4},{4,6},{6,8},{8,10},{10,12},{12,14},{14,16},{16,18},{18... | collective-permute-start | bytes 3145736 | tf_op jit(solution)/shard_map/ppermute | solution.py:15
  93.3 1.0 copy-start.6
  94.3 23.4 %collective-permute-start.3 = (bf16[2,8,64,512]{3,2,1,0:T(8,128)(2,1)S(1)}, bf16[2,8,64,512]{3,2,1,0:T(8,128)(2,1)S(1)}, u32[]{:S(2)}, u32[]{:S(2)}) collective-permute-start(bf16[2,8,64,512]{3,2,1,0:T(8,128)(2,1)S(1)} %collective-permute-done.2), channel_id=1, source_target_pairs={{0,2},{2,4},{4,6},{6,8},{8,10},{10,12},{12,14},{14,16},{16,18},{18... | collective-permute-start | bytes 3145736 | tf_op jit(solution)/shard_map/ppermute | solution.py:15
  117.7 1.0 copy-start.8
  118.7 22.5 %collective-permute-start.4 = (bf16[2,8,64,512]{3,2,1,0:T(8,128)(2,1)S(1)}, bf16[2,8,64,512]{3,2,1,0:T(8,128)(2,1)S(1)}, u32[]{:S(2)}, u32[]{:S(2)}) collective-permute-start(bf16[2,8,64,512]{3,2,1,0:T(8,128)(2,1)S(1)} %collective-permute-done.3), channel_id=1, source_target_pairs={{0,2},{2,4},{4,6},{6,8},{8,10},{10,12},{12,14},{14,16},{16,18},{18... | collective-permute-start | bytes 3145736 | tf_op jit(solution)/shard_map/ppermute | solution.py:15
  141.2 1.0 copy-start.10
  142.1 23.0 %collective-permute-start.5 = (bf16[2,8,64,512]{3,2,1,0:T(8,128)(2,1)S(1)}, bf16[2,8,64,512]{3,2,1,0:T(8,128)(2,1)S(1)}, u32[]{:S(2)}, u32[]{:S(2)}) collective-permute-start(bf16[2,8,64,512]{3,2,1,0:T(8,128)(2,1)S(1)} %collective-permute-done.4), channel_id=1, source_target_pairs={{0,2},{2,4},{4,6},{6,8},{8,10},{10,12},{12,14},{14,16},{16,18},{18... | collective-permute-start | bytes 3145736 | tf_op jit(solution)/shard_map/ppermute | solution.py:15
  165.1 1.0 copy-start.12
  166.1 22.9 %collective-permute-start.6 = (bf16[2,8,64,512]{3,2,1,0:T(8,128)(2,1)S(1)}, bf16[2,8,64,512]{3,2,1,0:T(8,128)(2,1)S(1)}, u32[]{:S(2)}, u32[]{:S(2)}) collective-permute-start(bf16[2,8,64,512]{3,2,1,0:T(8,128)(2,1)S(1)} %collective-permute-done.5), channel_id=1, source_target_pairs={{0,2},{2,4},{4,6},{6,8},{8,10},{10,12},{12,14},{14,16},{16,18},{18... | collective-permute-start | bytes 3145736 | tf_op jit(solution)/shard_map/ppermute | solution.py:15
  189.0 1.0 copy-start.14
  190.0 22.0 %collective-permute-start.7 = (bf16[2,8,64,512]{3,2,1,0:T(8,128)(2,1)S(1)}, bf16[2,8,64,512]{3,2,1,0:T(8,128)(2,1)}, u32[]{:S(2)}, u32[]{:S(2)}) collective-permute-start(bf16[2,8,64,512]{3,2,1,0:T(8,128)(2,1)S(1)} %collective-permute-done.6), channel_id=1, source_target_pairs={{0,2},{2,4},{4,6},{6,8},{8,10},{10,12},{12,14},{14,16},{16,18},{18... | collective-permute-start | bytes 3145736 | tf_op jit(solution)/shard_map/ppermute | solution.py:15
  212.0 21.7 %collective-permute-start.8 = (bf16[2,8,64,512]{3,2,1,0:T(8,128)(2,1)}, bf16[2,8,64,512]{3,2,1,0:T(8,128)(2,1)}, u32[]{:S(2)}, u32[]{:S(2)}) collective-permute-start(bf16[2,8,64,512]{3,2,1,0:T(8,128)(2,1)} %collective-permute-done.7), channel_id=1, source_target_pairs={{0,2},{2,4},{4,6},{6,8},{8,10},{10,12},{12,14},{14,16},{16,18},{18... | collective-permute-start | bytes 3145736 | tf_op jit(solution)/shard_map/ppermute | solution.py:15
  220.5 17.9 %copy-start.15 = (bf16[2,8,64,512]{3,2,1,0:T(8,128)(2,1)S(1)}, bf16[2,8,64,512]{3,2,1,0:T(8,128)(2,1)}, u32[]{:S(2)}) copy-start(bf16[2,8,64,512]{3,2,1,0:T(8,128)(2,1)} %copy-done.14) | copy-start | bytes 3145732
  220.6 18.9 %copy-start.13 = (bf16[2,8,64,512]{3,2,1,0:T(8,128)(2,1)S(1)}, bf16[2,8,64,512]{3,2,1,0:T(8,128)(2,1)}, u32[]{:S(2)}) copy-start(bf16[2,8,64,512]{3,2,1,0:T(8,128)(2,1)} %copy-done.12) | copy-start | bytes 3145732
  220.6 20.0 %copy-start.11 = (bf16[2,8,64,512]{3,2,1,0:T(8,128)(2,1)S(1)}, bf16[2,8,64,512]{3,2,1,0:T(8,128)(2,1)}, u32[]{:S(2)}) copy-start(bf16[2,8,64,512]{3,2,1,0:T(8,128)(2,1)} %copy-done.10) | copy-start | bytes 3145732
  236.0 5.6 %copy-start.9 = (bf16[2,8,64,512]{3,2,1,0:T(8,128)(2,1)S(1)}, bf16[2,8,64,512]{3,2,1,0:T(8,128)(2,1)}, u32[]{:S(2)}) copy-start(bf16[2,8,64,512]{3,2,1,0:T(8,128)(2,1)} %copy-done.8) | copy-start | bytes 3145732
  238.4 4.3 %copy-start.7 = (bf16[2,8,64,512]{3,2,1,0:T(8,128)(2,1)S(1)}, bf16[2,8,64,512]{3,2,1,0:T(8,128)(2,1)}, u32[]{:S(2)}) copy-start(bf16[2,8,64,512]{3,2,1,0:T(8,128)(2,1)} %copy-done.6) | copy-start | bytes 3145732
  239.5 4.4 %copy-start.5 = (bf16[2,8,64,512]{3,2,1,0:T(8,128)(2,1)S(1)}, bf16[2,8,64,512]{3,2,1,0:T(8,128)(2,1)}, u32[]{:S(2)}) copy-start(bf16[2,8,64,512]{3,2,1,0:T(8,128)(2,1)} %copy-done.4) | copy-start | bytes 3145732
  240.6 4.4 %copy-start.2 = (bf16[3,8,64,512]{3,2,1,0:T(8,128)(2,1)S(1)}, bf16[3,8,64,512]{3,2,1,0:T(8,128)(2,1)}, u32[]{:S(2)}) copy-start(bf16[3,8,64,512]{3,2,1,0:T(8,128)(2,1)} %copy-done.1) | copy-start | bytes 4718596
Sparse Core Ops, SparseCore 0:
  287.5 55.1 reduce-scatter.1
where the time goes:
time: 353 us; the launch traced here: 352 us
  waiting for transfers between devices  212 us (60%)
  local copies, waits for them, and re-layouts  47.9 us (14%)
  starting transfers between devices  46.7 us (13%)
  matrix products  20 us (6%)
  between operations  13.6 us (4%)
  other arithmetic  11.7 us (3%)
    ppermute x9, waiting for transfers between devices, shifted_2(): lax.ppermute(value, axis, [(source, source + steps) for source in range(f...  157 us
    reduce_scatter x1, waiting for transfers between devices, shards(): lax.psum_scatter(partial_value, 'head', scatter_dimension=2, tiled=True)  55.3 us
    ppermute x9, starting transfers between devices, shifted_2(): lax.ppermute(value, axis, [(source, source + steps) for source in range(f...  46.7 us
    unnamed x46, local copies, waits for them, and re-layouts  19.9 us
    slice x1, local copies, waits for them, and re-layouts, shards(): window[0]  8.85 us
    another operation x1, local copies, waits for them, and re-layouts, attend(): key_heads = keys_in.reshape(key_len, positions, head_count, head_dim)  7.7 us
    another operation x1, local copies, waits for them, and re-layouts, attend(): value_heads = values_in.reshape(key_len, positions, head_count, head_dim)  7.69 us
    sub x1, matrix products, attend(): unnorm = jnp.where(allowed[None, None], jnp.exp(masked - row_max), 0.0)  7.39 us
  transfers between devices with their start and end apart: 10, of which 10 were waited for; matrix products, arithmetic and copies ran while one was open for 0% of the time, Pallas kernels for 0%

commit v1 on v0

v1 whole, which is shorter than its diff:
```python
import functools
import math

import jax
import jax.numpy as jnp
from jax import lax
from jax.experimental import pallas as pl
from jax.experimental.pallas import tpu as pltpu
from jax.sharding import Mesh
from jax.sharding import PartitionSpec as P

HEAD_DIM = 128
BACK = 64
PLANES, ROWS, COLS, CORES = 4, 8, 4, 2
GROUP = ROWS * COLS
LANES = 128
QUERY_BLOCK = 128
SWAP = [(0, 1), (1, 0)]


def attention_kernel(main_own, main_other, halo_own, halo_other, lag_ref, taps_ref, out_ref, pad, conv):
    frames = main_own.shape[1]
    total = BACK + frames
    half = main_own.shape[2]
    lag = lag_ref[...].astype(jnp.float32)
    pad[0:8] = jnp.zeros((8, half), jnp.float32)
    for side, (main, halo) in enumerate(((main_own, halo_own), (main_other, halo_other))):
        for kind in range(3):
            pad[8 : 8 + BACK] = halo[kind]
            pad[8 + BACK : 8 + total] = main[kind]
            for column in range(0, half, LANES):
                columns = slice(column, column + LANES)
                acc = taps_ref[side, 0, kind, columns][None, :] * pad[8 : 8 + total, columns]
                for frame_lag in (1, 2):
                    term = (
                        taps_ref[side, frame_lag, kind, columns][None, :]
                        * pad[8 - frame_lag : 8 - frame_lag + total, columns]
                    )
                    acc = acc + jnp.where(lag >= frame_lag, term, 0.0)
                conv[kind, :, side * half + column : side * half + column + LANES] = acc.astype(
                    jnp.bfloat16
                )
    keys = QUERY_BLOCK + BACK
    row = lax.broadcasted_iota(jnp.int32, (QUERY_BLOCK, keys), 0)
    col = lax.broadcasted_iota(jnp.int32, (QUERY_BLOCK, keys), 1)
    age = row + BACK - col
    for block in range(frames // QUERY_BLOCK):
        first = block * QUERY_BLOCK
        query_lag = lag_ref[BACK + first : BACK + first + QUERY_BLOCK, 0:1].astype(jnp.int32)
        allowed = (age >= 0) & (age <= query_lag)
        for head in range(2 * half // HEAD_DIM):
            columns = slice(head * HEAD_DIM, (head + 1) * HEAD_DIM)
            query = conv[0, BACK + first : BACK + first + QUERY_BLOCK, columns]
            key = conv[1, first : first + keys, columns]
            value = conv[2, first : first + keys, columns]
            scores = lax.dot_general(
                query, key, (((1,), (1,)), ((), ())), preferred_element_type=jnp.float32
            ) / math.sqrt(HEAD_DIM)
            masked = jnp.where(allowed, scores, -1e30)
            unnorm = jnp.exp(masked - jnp.max(masked, axis=-1, keepdims=True))
            unnorm = jnp.where(allowed, unnorm, 0.0)
            probs = (unnorm / jnp.sum(unnorm, axis=-1, keepdims=True)).astype(jnp.bfloat16)
            result = jnp.dot(probs, value, preferred_element_type=jnp.float32)
            out_ref[first : first + QUERY_BLOCK, columns] = result.astype(jnp.bfloat16)


def attention(main_own, main_other, halo_own, halo_other, lag, taps):
    frames, half = main_own.shape[1:]
    vmem = pl.BlockSpec(memory_space=pltpu.VMEM)
    return pl.pallas_call(
        attention_kernel,
        out_shape=jax.ShapeDtypeStruct((frames, 2 * half), jnp.bfloat16),
        in_specs=[vmem] * 6,
        out_specs=vmem,
        scratch_shapes=[
            pltpu.VMEM((8 + BACK + frames, half), jnp.float32),
            pltpu.VMEM((3, BACK + frames, 2 * half), jnp.bfloat16),
        ],
    )(main_own, main_other, halo_own, halo_other, lag, taps)


def shards(tokens, w_qkv, conv_taps, w_out, episode_start):
    frames, positions, model_width = tokens.shape
    inner_width = w_qkv.shape[2]
    share = positions // CORES
    core = lax.axis_index("core")
    device_row = lax.axis_index(("y", "z", "x"))
    out_half = model_width // CORES

    w_other = lax.ppermute(w_qkv, "core", SWAP)
    taps_other = lax.ppermute(conv_taps, "core", SWAP)
    mine = lax.dynamic_slice_in_dim(w_out, core * out_half, out_half, 1)
    theirs = lax.dynamic_slice_in_dim(w_out, (1 - core) * out_half, out_half, 1)
    w_out_other = lax.ppermute(theirs, "core", SWAP)

    tokens_f = lax.dynamic_slice_in_dim(tokens, core * share, share, 1).astype(jnp.float32)
    inv_rms = lax.rsqrt(jnp.mean(tokens_f * tokens_f, axis=-1, keepdims=True) + 1e-06)
    normed = (tokens_f * inv_rms).astype(jnp.bfloat16).transpose(1, 0, 2)
    frame_ids = device_row * frames + jnp.arange(frames, dtype=jnp.int32)
    lag = (frame_ids - episode_start).astype(jnp.bfloat16)
    packed = jnp.concatenate(
        [normed, jnp.broadcast_to(lag[None, :, None], (share, frames, LANES))], axis=2
    )
    rows = lax.all_to_all(packed, ("z", "x"), 0, 0, tiled=True)
    rows = rows.reshape(GROUP * frames, model_width + LANES)
    halo = lax.ppermute(rows[-BACK:], "y", [(y, y + 1) for y in range(PLANES - 1)])

    def project(part, weight):
        return jnp.einsum(
            "nd,cde->cne", part[:, :model_width], weight, preferred_element_type=jnp.float32
        )

    attended = attention(
        project(rows, w_qkv),
        project(rows, w_other),
        project(halo, w_qkv),
        project(halo, w_other),
        jnp.concatenate([halo[:, model_width:], rows[:, model_width:]], axis=0),
        jnp.stack([conv_taps, taps_other]),
    )
    back = lax.all_to_all(
        attended.reshape(GROUP, frames, CORES * inner_width), ("z", "x"), 0, 0, tiled=True
    )
    back_other = lax.ppermute(back, "core", SWAP)

    def output(part, first, second):
        flat = part.reshape(share * frames, CORES * inner_width)
        return (
            jnp.dot(flat[:, :inner_width], first, preferred_element_type=jnp.float32)
            + jnp.dot(flat[:, inner_width:], second, preferred_element_type=jnp.float32)
        ).astype(jnp.bfloat16).reshape(share, frames, out_half).transpose(1, 0, 2)

    out_mine = output(back, mine, w_out_other)
    out_other = output(back_other, w_out_other, mine)
    result = jnp.zeros((frames, positions, out_half), jnp.bfloat16)
    result = lax.dynamic_update_slice_in_dim(result, out_mine, core * share, 1)
    return lax.dynamic_update_slice_in_dim(result, out_other, (1 - core) * share, 1)


def solution(mesh):
    grid = Mesh(mesh.devices.reshape(PLANES, ROWS, COLS, CORES), ("y", "z", "x", "core"))
    seq = ("y", "z", "x")
    in_specs = (
        P(seq, None, None),
        P(None, None, "core"),
        P(None, None, "core"),
        P("core", None),
        P(seq),
    )
    return jax.shard_map(
        shards, mesh=grid, in_specs=in_specs, out_specs=P(seq, None, "core"), check_vma=False
    )
```

time: 353 us -> 106 us (0.30)
  waiting for transfers between devices: 212 us -> 38.7 us
  local copies, waits for them, and re-layouts: 47.9 us -> 4.1 us
  starting transfers between devices: 46.7 us -> 28.5 us
  between operations: 13.6 us -> 0.16 us
  Pallas kernels: 0 us -> 8.53 us
  other arithmetic: 11.7 us -> 3.7 us
    ppermute x9 -> x5, waiting for transfers between devices: 157 us -> 0.86 us  [the longest x1 0.85 us: shards(): taps_other = lax.ppermute(conv_taps, 'core', SWAP)]
    reduce_scatter x1 -> x0, waiting for transfers between devices: 55.3 us -> none  [shards(): lax.psum_scatter(partial_value, 'head', scatter_dimension=2, tiled=True)]
    all_to_all x0 -> x2, waiting for transfers between devices: none -> 37.9 us  [the longest x1 26.4 us: shards(): rows = lax.all_to_all(packed, ('z', 'x'), 0, 0, tiled=True)]
    ppermute x9 -> x5, starting transfers between devices: 46.7 us -> 13.5 us  [the longest x1 4.06 us: shards(): back_other = lax.ppermute(back, 'core', SWAP)]
    unnamed x46 -> x12, local copies, waits for them, and re-layouts: 19.9 us -> 0.08 us
    another operation x3 -> x0, local copies, waits for them, and re-layouts: 15.5 us -> none  [the longest x1 7.7 us: attend(): key_heads = keys_in.reshape(key_len, positions, head_count, head_dim)]
    all_to_all x0 -> x2, starting transfers between devices: none -> 15 us  [the longest x1 9.33 us: shards(): rows = lax.all_to_all(packed, ('z', 'x'), 0, 0, tiled=True)]
    slice x4 -> x3, local copies, waits for them, and re-layouts: 10.9 us -> 0.03 us  [the longest x1 0.02 us: shards(): rows[-BACK:]]
  transfers between devices with their start and end apart: 10 -> 7, of which waited for: 10 -> 3; matrix products, arithmetic and copies ran while one was open for 0% -> 16% of each run, Pallas kernels for 0% -> 0%
where the time goes in v1:
time: 106 us
  waiting for transfers between devices  38.7 us (37%)
  starting transfers between devices  28.5 us (27%)
  matrix products  22 us (21%)
  Pallas kernels  8.53 us (8%)
  local copies, waits for them, and re-layouts  4.1 us (4%)
  other arithmetic  3.7 us (3%)
    all_to_all x1, waiting for transfers between devices, shards(): rows = lax.all_to_all(packed, ('z', 'x'), 0, 0, tiled=True)  26.4 us
    dot_general x4, matrix products, project(): jnp.einsum('nd,cde->cne', part[:, :model_width], weight, preferred_elemen...  18.4 us
    all_to_all x1, waiting for transfers between devices, shards(): lax.all_to_all(attended.reshape(GROUP, frames, CORES * inner_width), ('z'...  11.4 us
    all_to_all x1, starting transfers between devices, shards(): rows = lax.all_to_all(packed, ('z', 'x'), 0, 0, tiled=True)  9.33 us
    pallas_call x1, Pallas kernels, attention(): pl.pallas_call(attention_kernel, out_shape=jax.ShapeDtypeStruct((frames,...  8.53 us
    all_to_all x1, starting transfers between devices, shards(): lax.all_to_all(attended.reshape(GROUP, frames, CORES * inner_width), ('z'...  5.69 us
    ppermute x1, starting transfers between devices, shards(): back_other = lax.ppermute(back, 'core', SWAP)  4.06 us
    ppermute x1, starting transfers between devices, shards(): lax.ppermute(rows[-BACK:], 'y', [(y, y + 1) for y in range(PLANES - 1)])  3.48 us
  transfers between devices with their start and end apart: 7, of which 3 were waited for; matrix products, arithmetic and copies ran while one was open for 16% of the time, Pallas kernels for 0%

profile of v1, /device:TPU:1, one launch (start us, length us, event | category | flops | bytes accessed | tf_op | source)
XLA Modules:
  0.0 105.8 jit_solution(2948884587385164913)
XLA Ops:
  0.0 0.0 copy-start
  0.0 0.0 copy-start.3
  0.0 3.2 %collective-permute-start = (bf16[3,2048,512]{2,1,0:T(8,128)(2,1)}, bf16[3,2048,512]{2,1,0:T(8,128)(2,1)}, u32[]{:S(2)}, u32[]{:S(2)}) collective-permute-start(bf16[3,2048,512]{2,1,0:T(8,128)(2,1)} %param.6), channel_id=1, source_target_pairs={{0,1},{1,0},{2,3},{3,2},{4,5},{5,4},{6,7},{7,6},{8,9},{9,8},{10,11... | collective-permute-start | bytes 18874376 | tf_op jit(solution)/shard_map/ppermute | solution.py:90
  3.2 1.3 %constant_dynamic-slice_fusion.1 = bf16[8,32,2048]{2,1,0:T(8,128)(2,1)S(1)} fusion(bf16[8,64,2048]{2,1,0:T(8,128)(2,1)} %param.5, s32[]{:T(128)S(6)} %select_n.13), kind=kLoop, calls=%fused_computation.35 | loop fusion | bytes 2097156 | tf_op jit(solution)/shard_map/dynamic_slice | solution.py:96
  4.5 0.7 fusion
  5.2 0.0 copy-done.3
  5.3 0.6 fusion.6
  5.9 0.1 broadcast_in_dim.5
  6.0 0.0 copy-start.2
  6.0 1.1 %pad_maximum_fusion = bf16[32,8,2176]{2,1,0:T(8,128)(2,1)} fusion(bf16[32,8,128]{2,1,0:T(8,128)(2,1)S(1)} %broadcast_in_dim.5, bf16[32,8,2048]{2,1,0:T(8,128)(2,1)S(1)} %fusion.6), kind=kLoop, calls=%fused_computation.14 | loop fusion | flops 2228224 | bytes 2228224 | tf_op jit(solution)/shard_map/concatenate | solution.py:101
  7.1 9.3 %all-to-all-start = ((bf16[32,8,2176]{2,1,0:T(8,128)(2,1)}), bf16[32,8,2176]{2,1,0:T(8,128)(2,1)S(1)}, u32[]{:S(2)}, u32[]{:S(2)}) async-start(bf16[32,8,2176]{2,1,0:T(8,128)(2,1)} %pad_maximum_fusion), calls=%async_computation | async-start | bytes 2228224 | tf_op jit(solution)/shard_map/all_to_all | solution.py:104
  16.4 0.0 copy-done.2
  16.4 0.5 collective-permute-start.2
  17.0 0.8 collective-permute-done.2
  17.8 0.6 pad_maximum_fusion.2.taps_ref
  18.4 26.4 %all-to-all-done = bf16[32,8,2176]{2,1,0:T(8,128)(2,1)S(1)} async-done(((bf16[32,8,2176]{2,1,0:T(8,128)(2,1)}), bf16[32,8,2176]{2,1,0:T(8,128)(2,1)S(1)}, u32[]{:S(2)}, u32[]{:S(2)}) %all-to-all-start) | async-done | bytes 1114144 | tf_op jit(solution)/shard_map/all_to_all | solution.py:104
  44.9 0.0 slice-start
  44.9 3.5 %collective-permute-start.1 = (bf16[64,2176]{1,0:T(8,128)(2,1)S(1)}, bf16[64,2176]{1,0:T(8,128)(2,1)S(1)}, u32[]{:S(2)}, u32[]{:S(2)}) collective-permute-start(bf16[64,2176]{1,0:T(8,128)(2,1)S(1)} %slice_bitcast_fusion.3), channel_id=1, source_target_pairs={{0,64},{64,128},{128,192},{1,65},{65,129},{129,193},{2,66},{66,130... | collective-permute-start | bytes 835592 | tf_op jit(solution)/shard_map/ppermute | solution.py:106
  48.4 0.0 slice-start.1
  48.4 5.9 %convolution_bitcast_fusion.1.main_own = f32[3,256,512]{2,1,0:T(8,128)} fusion(bf16[3,2048,512]{2,1,0:T(8,128)(2,1)} %param.6, bf16[256,2176]{1,0:T(8,128)(2,1)S(1)} %bitcast.43), kind=kOutput, calls=%fused_computation.5 | convolution fusion | flops 1610612736 | bytes 8912896 | tf_op jit(solution)/shard_map/nd,cde->cne/dot_general | solution.py:109
  54.3 0.0 collective-permute-done.1
  54.3 0.6 pad_maximum_fusion.1.lag_ref
  54.9 0.0 slice-done
  54.9 0.0 slice-done.1
  54.9 1.9 %convolution_bitcast_fusion.3.halo_own = f32[3,64,512]{2,1,0:T(8,128)} fusion(bf16[3,2048,512]{2,1,0:T(8,128)(2,1)S(1)} %bitcast.41, bf16[64,2176]{1,0:T(8,128)(2,1)S(1)} %collective-permute-done.1), kind=kOutput, calls=%fused_computation.13 | convolution fusion | flops 402653184 | bytes 6946816 | tf_op jit(solution)/shard_map/nd,cde->cne/dot_general | solution.py:109
  56.9 0.0 collective-permute-done
  56.9 5.8 %convolution_bitcast_fusion.main_other = f32[3,256,512]{2,1,0:T(8,128)} fusion(bf16[3,2048,512]{2,1,0:T(8,128)(2,1)} %collective-permute-done, bf16[256,2176]{1,0:T(8,128)(2,1)S(1)} %bitcast.45), kind=kOutput, calls=%fused_computation.4 | convolution fusion | flops 1610612736 | bytes 8912896 | tf_op jit(solution)/shard_map/nd,cde->cne/dot_general | solution.py:109
  62.7 4.7 %convolution_bitcast_fusion.2.halo_other = f32[3,64,512]{2,1,0:T(8,128)} fusion(bf16[3,2048,512]{2,1,0:T(8,128)(2,1)} %collective-permute-done, bf16[64,2176]{1,0:T(8,128)(2,1)S(1)} %collective-permute-done.1), kind=kOutput, calls=%fused_computation.12 | convolution fusion | flops 402653184 | bytes 6946816 | tf_op jit(solution)/shard_map/nd,cde->cne/dot_general | solution.py:109
  67.4 8.5 %shard_map.55 = bf16[256,1024]{1,0:T(8,128)(2,1)} custom-call(f32[3,256,512]{2,1,0:T(8,128)} %convolution_bitcast_fusion.1.main_own, f32[3,256,512]{2,1,0:T(8,128)} %convolution_bitcast_fusion.main_other, f32[3,64,512]{2,1,0:T(8,128)} %convolution_bitcast_fusion.3.halo_own, f32[3,64,512]{2,1,0:T(8,128)} %convolution_bitcast_fusion.2.halo_other, ...), custom_call_target="tpu_custom_call" | custom-call | tf_op jit(solution)/shard_map/pallas_call | solution.py:70
  76.0 5.7 %all-to-all-start.1 = ((bf16[32,8,1024]{2,1,0:T(8,128)(2,1)}), bf16[32,8,1024]{2,1,0:T(8,128)(2,1)}, u32[]{:S(2)}, u32[]{:S(2)}) async-start(bf16[32,8,1024]{2,1,0:T(8,128)(2,1)} %bitcast.42), calls=%async_computation.1 | async-start | bytes 1048576 | tf_op jit(solution)/shard_map/all_to_all | solution.py:121
  81.7 0.0 copy-done
  81.7 1.1 %constant_dynamic-slice_fusion = bf16[512,1024]{1,0:T(8,128)(2,1)} fusion(bf16[512,2048]{1,0:T(8,128)(2,1)S(1)} %copy-done, s32[]{:T(128)S(6)} %select_n.15), kind=kLoop, calls=%fused_computation.33 | loop fusion | bytes 2097156 | tf_op jit(solution)/shard_map/dynamic_slice | solution.py:93
  82.8 2.2 %collective-permute-start.3 = (bf16[512,1024]{1,0:T(8,128)(2,1)}, bf16[512,1024]{1,0:T(8,128)(2,1)S(1)}, u32[]{:S(2)}, u32[]{:S(2)}) collective-permute-start(bf16[512,1024]{1,0:T(8,128)(2,1)} %constant_dynamic-slice_fusion), channel_id=1, source_target_pairs={{0,1},{1,0},{2,3},{3,2},{4,5},{5,4},{6,7},{7,6},{8,9},{9,8},{10,11... | collective-permute-start | bytes 3145736 | tf_op jit(solution)/shard_map/ppermute | solution.py:94
  85.0 11.4 %all-to-all-done.1 = bf16[32,8,1024]{2,1,0:T(8,128)(2,1)} async-done(((bf16[32,8,1024]{2,1,0:T(8,128)(2,1)}), bf16[32,8,1024]{2,1,0:T(8,128)(2,1)}, u32[]{:S(2)}, u32[]{:S(2)}) %all-to-all-start.1) | async-done | bytes 524320 | tf_op jit(solution)/shard_map/all_to_all | solution.py:121
  96.4 4.1 %collective-permute-start.4 = (bf16[32,8,1024]{2,1,0:T(8,128)(2,1)}, bf16[32,8,1024]{2,1,0:T(8,128)(2,1)S(1)}, u32[]{:S(2)}, u32[]{:S(2)}) collective-permute-start(bf16[32,8,1024]{2,1,0:T(8,128)(2,1)} %all-to-all-done.1), channel_id=1, source_target_pairs={{0,1},{1,0},{2,3},{3,2},{4,5},{5,4},{6,7},{7,6},{8,9},{9,8},{10,11... | collective-permute-start | bytes 1572872 | tf_op jit(solution)/shard_map/ppermute | solution.py:124
  100.5 1.4 %fusion.9 = f32[256,1024]{1,0:T(8,128)S(1)} fusion(bf16[512,2048]{1,0:T(8,128)(2,1)S(1)} %copy-done, s32[]{:T(128)S(6)} %select_n.14, bf16[256,1024]{1,0:T(8,128)(2,1)} %bitcast.12), kind=kOutput, calls=%fused_computation.19 | convolution fusion | flops 268435456 | bytes 2359300 | tf_op jit(solution)/shard_map/dot_general | solution.py:129
  101.8 0.0 collective-permute-done.3
  101.9 1.4 %fusion.5 = bf16[32,8,1024]{2,1,0:T(8,128)(2,1)S(1)} fusion(f32[256,1024]{1,0:T(8,128)S(1)} %fusion.9, bf16[512,1024]{1,0:T(8,128)(2,1)S(1)} %collective-permute-done.3, bf16[256,1024]{1,0:T(8,128)(2,1)} %bitcast.12), kind=kOutput, calls=%fused_computation.11 | convolution fusion | flops 268959744 | bytes 2883584 | tf_op jit(solution)/shard_map/dot_general | solution.py:130
  103.3 0.1 broadcast_in_dim.4
  103.4 0.3 bitcast_dynamic-update-slice_fusion.1
  103.7 0.0 copy-start.1
  103.7 0.0 collective-permute-done.4
  103.7 0.4 fusion.7
  104.2 0.4 fusion.4
  104.6 0.0 copy-done.1
  104.7 1.1 %bitcast_dynamic-update-slice_fusion = bf16[8,64,1024]{2,1,0:T(8,128)(2,1)} fusion(bf16[8,64,1024]{2,1,0:T(8,128)(2,1)} %copy-done.1, s32[]{:T(128)S(6)} %select_n.16, bf16[32,8,1024]{2,1,0:T(8,128)(2,1)S(1)} %fusion.4), kind=kLoop, calls=%fused_computation.21 | loop fusion | bytes 1048580 | tf_op jit(solution)/shard_map/dynamic_update_slice | solution.py:137
  (6 shorter events, 0.0 us)
Async XLA Ops:
  0.0 81.7 %copy-start = (bf16[512,2048]{1,0:T(8,128)(2,1)S(1)}, bf16[512,2048]{1,0:T(8,128)(2,1)}, u32[]{:S(2)}) copy-start(bf16[512,2048]{1,0:T(8,128)(2,1)} %param.8) | copy-start | bytes 6291460
  0.0 5.2 %copy-start.3 = (s32[8]{0:T(128)S(1)}, s32[8]{0:T(128)}, u32[]{:S(2)}) copy-start(s32[8]{0:T(128)} %param.9) | copy-start | bytes 100
  0.0 56.9 %collective-permute-start = (bf16[3,2048,512]{2,1,0:T(8,128)(2,1)}, bf16[3,2048,512]{2,1,0:T(8,128)(2,1)}, u32[]{:S(2)}, u32[]{:S(2)}) collective-permute-start(bf16[3,2048,512]{2,1,0:T(8,128)(2,1)} %param.6), channel_id=1, source_target_pairs={{0,1},{1,0},{2,3},{3,2},{4,5},{5,4},{6,7},{7,6},{8,9},{9,8},{10,11... | collective-permute-start | bytes 18874376 | tf_op jit(solution)/shard_map/ppermute | solution.py:90
  6.0 10.4 %copy-start.2 = (f32[3,3,512]{2,1,0:T(4,128)S(1)}, f32[3,3,512]{2,1,0:T(4,128)}, u32[]{:S(2)}) copy-start(f32[3,3,512]{2,1,0:T(4,128)} %param.7) | copy-start | bytes 55300
  7.1 37.8 %all-to-all-start = ((bf16[32,8,2176]{2,1,0:T(8,128)(2,1)}), bf16[32,8,2176]{2,1,0:T(8,128)(2,1)S(1)}, u32[]{:S(2)}, u32[]{:S(2)}) async-start(bf16[32,8,2176]{2,1,0:T(8,128)(2,1)} %pad_maximum_fusion), calls=%async_computation | async-start | bytes 2228224 | tf_op jit(solution)/shard_map/all_to_all | solution.py:104
  16.4 1.4 %collective-permute-start.2 = (f32[3,3,512]{2,1,0:T(4,128)S(1)}, f32[3,3,512]{2,1,0:T(4,128)S(1)}, u32[]{:S(2)}, u32[]{:S(2)}) collective-permute-start(f32[3,3,512]{2,1,0:T(4,128)S(1)} %copy-done.2), channel_id=1, source_target_pairs={{0,1},{1,0},{2,3},{3,2},{4,5},{5,4},{6,7},{7,6},{8,9},{9,8},{10,11... | collective-permute-start | bytes 55304 | tf_op jit(solution)/shard_map/ppermute | solution.py:91
  44.9 10.1 %slice-start = ((s8[6291456]{0:T(1024)(128)(4,1)}), s8[4194304]{0:T(1024)(128)(4,1)S(1)}, s32[]{:S(2)}) async-start(s8[6291456]{0:T(1024)(128)(4,1)} %bitcast.40), calls=%async_computation.2 | async-start | bytes 8388608
  44.9 9.4 %collective-permute-start.1 = (bf16[64,2176]{1,0:T(8,128)(2,1)S(1)}, bf16[64,2176]{1,0:T(8,128)(2,1)S(1)}, u32[]{:S(2)}, u32[]{:S(2)}) collective-permute-start(bf16[64,2176]{1,0:T(8,128)(2,1)S(1)} %slice_bitcast_fusion.3), channel_id=1, source_target_pairs={{0,64},{64,128},{128,192},{1,65},{65,129},{129,193},{2,66},{66,130... | collective-permute-start | bytes 835592 | tf_op jit(solution)/shard_map/ppermute | solution.py:106
  48.4 6.5 %slice-start.1 = ((s8[6291456]{0:T(1024)(128)(4,1)}), s8[2097152]{0:T(1024)(128)(4,1)S(1)}, s32[]{:S(2)}) async-start(s8[6291456]{0:T(1024)(128)(4,1)} %bitcast.40), calls=%async_computation.3 | async-start | bytes 4194304
  76.0 20.4 %all-to-all-start.1 = ((bf16[32,8,1024]{2,1,0:T(8,128)(2,1)}), bf16[32,8,1024]{2,1,0:T(8,128)(2,1)}, u32[]{:S(2)}, u32[]{:S(2)}) async-start(bf16[32,8,1024]{2,1,0:T(8,128)(2,1)} %bitcast.42), calls=%async_computation.1 | async-start | bytes 1048576 | tf_op jit(solution)/shard_map/all_to_all | solution.py:121
  82.8 19.1 %collective-permute-start.3 = (bf16[512,1024]{1,0:T(8,128)(2,1)}, bf16[512,1024]{1,0:T(8,128)(2,1)S(1)}, u32[]{:S(2)}, u32[]{:S(2)}) collective-permute-start(bf16[512,1024]{1,0:T(8,128)(2,1)} %constant_dynamic-slice_fusion), channel_id=1, source_target_pairs={{0,1},{1,0},{2,3},{3,2},{4,5},{5,4},{6,7},{7,6},{8,9},{9,8},{10,11... | collective-permute-start | bytes 3145736 | tf_op jit(solution)/shard_map/ppermute | solution.py:94
  96.4 7.3 %collective-permute-start.4 = (bf16[32,8,1024]{2,1,0:T(8,128)(2,1)}, bf16[32,8,1024]{2,1,0:T(8,128)(2,1)S(1)}, u32[]{:S(2)}, u32[]{:S(2)}) collective-permute-start(bf16[32,8,1024]{2,1,0:T(8,128)(2,1)} %all-to-all-done.1), channel_id=1, source_target_pairs={{0,1},{1,0},{2,3},{3,2},{4,5},{5,4},{6,7},{7,6},{8,9},{9,8},{10,11... | collective-permute-start | bytes 1572872 | tf_op jit(solution)/shard_map/ppermute | solution.py:124
  103.7 1.0 copy-start.1

commit v2 on v1

v2 whole, which is shorter than its diff:
```python
import functools
import math

import jax
import jax.numpy as jnp
from jax import lax
from jax.experimental import pallas as pl
from jax.experimental.pallas import tpu as pltpu
from jax.sharding import Mesh
from jax.sharding import PartitionSpec as P

HEAD_DIM = 128
BACK = 64
PLANES, ROWS, COLS, CORES = 4, 8, 4, 2
GROUP = ROWS * COLS
LANES = 128
PAIR = 256
LIMIT = 12 * 1024 * 1024
SWAP = [(0, 1), (1, 0)]


def convolve(pad, conv, taps_ref, masks, kind, first_column, rows):
    for column in range(0, PAIR, LANES):
        columns = slice(column, column + LANES)
        taps = slice(first_column + column, first_column + column + LANES)
        acc = taps_ref[0, kind, taps][None, :] * pad[8 : 8 + rows, columns]
        for lag in (1, 2):
            acc = acc + (
                taps_ref[lag, kind, taps][None, :] * pad[8 - lag : 8 - lag + rows, columns]
            ) * masks[lag - 1]
        conv[kind, :, columns] = acc.astype(jnp.bfloat16)


def attend(query, key, value, bias):
    scores = lax.dot_general(
        query, key, (((1,), (1,)), ((), ())), preferred_element_type=jnp.float32
    )
    masked = scores * (1.0 / math.sqrt(HEAD_DIM)) + bias
    unnorm = jnp.exp(masked - jnp.max(masked, axis=-1, keepdims=True))
    probs = unnorm * (1.0 / jnp.sum(unnorm, axis=-1, keepdims=True))
    return jnp.dot(
        probs.astype(jnp.bfloat16), value, preferred_element_type=jnp.float32
    ).astype(jnp.bfloat16)


def mask_bias(query_lag, first_query, queries, keys):
    row = lax.broadcasted_iota(jnp.int32, (queries, keys), 0)
    col = lax.broadcasted_iota(jnp.int32, (queries, keys), 1)
    age = (row + first_query - col).astype(jnp.float32)
    return jnp.where((age >= 0) & (age <= query_lag), 0.0, -1e30)


def weight_of(own, other, pair, kind):
    per_side = own.shape[2] // PAIR
    side = own if pair < per_side else other
    first = (pair % per_side) * PAIR
    return side[kind, :, first : first + PAIR]


def main_kernel(x_ref, own, other, taps_own, taps_other, out_ref, first_ref, pad0, pad1, conv0, conv1, mask_ref, bias_ref):
    frames = x_ref.shape[0]
    width = own.shape[1]
    per_side = own.shape[2] // PAIR
    lag = x_ref[:, width : width + LANES].astype(jnp.float32)
    for step in (1, 2):
        mask_ref[step - 1] = (lag >= step).astype(jnp.float32)
    bias_ref[...] = mask_bias(lag[BACK:, 0:1], BACK, frames - BACK, frames)
    pads, convs, taps = (pad0, pad1), (conv0, conv1), (taps_own, taps_other)
    for pad in pads:
        for kind in range(3):
            pad[kind, 0:8] = jnp.zeros((8, PAIR), jnp.float32)
    for pair in range(2 * per_side + 1):
        if pair < 2 * per_side:
            pad, conv = pads[pair % 2], convs[pair % 2]
            for kind in range(3):
                projected = jnp.dot(
                    x_ref[:, :width], weight_of(own, other, pair, kind), preferred_element_type=jnp.float32
                )
                pad[kind, 8 : 8 + frames] = projected
                first_ref[kind, :, pair * PAIR : (pair + 1) * PAIR] = projected[:BACK]
                convolve(
                    pad.at[kind], conv, taps[pair // per_side], mask_ref, kind,
                    (pair % per_side) * PAIR, frames,
                )
        if pair > 0:
            conv = convs[(pair - 1) % 2]
            for head in range(PAIR // HEAD_DIM):
                columns = slice(head * HEAD_DIM, (head + 1) * HEAD_DIM)
                start = (pair - 1) * PAIR + head * HEAD_DIM
                out_ref[BACK:, start : start + HEAD_DIM] = attend(
                    conv[0, BACK:, columns], conv[1, :, columns], conv[2, :, columns], bias_ref[...]
                )


def halo_kernel(x_ref, lag_ref, own, other, taps_own, taps_other, first_ref, done_ref, out_ref, pad0, pad1, conv0, conv1, mask_ref, bias_ref, result, out_sem):
    del done_ref
    rows = 2 * BACK
    width = own.shape[1]
    per_side = own.shape[2] // PAIR
    halo_lag = x_ref[:, width : width + LANES].astype(jnp.float32)
    lag = lag_ref[...].astype(jnp.float32)
    for step in (1, 2):
        mask_ref[step - 1, :BACK] = (halo_lag >= step).astype(jnp.float32)
        mask_ref[step - 1, BACK:] = (lag >= step).astype(jnp.float32)
    bias_ref[...] = mask_bias(lag[:, 0:1], BACK, BACK, rows)
    pads, convs, taps = (pad0, pad1), (conv0, conv1), (taps_own, taps_other)
    for pad in pads:
        for kind in range(3):
            pad[kind, 0:8] = jnp.zeros((8, PAIR), jnp.float32)
    for pair in range(2 * per_side + 1):
        if pair < 2 * per_side:
            pad, conv = pads[pair % 2], convs[pair % 2]
            for kind in range(3):
                pad[kind, 8 : 8 + BACK] = jnp.dot(
                    x_ref[:, :width], weight_of(own, other, pair, kind), preferred_element_type=jnp.float32
                )
                pad[kind, 8 + BACK : 8 + rows] = first_ref[kind, :, pair * PAIR : (pair + 1) * PAIR]
                convolve(
                    pad.at[kind], conv, taps[pair // per_side], mask_ref, kind,
                    (pair % per_side) * PAIR, rows,
                )
        if pair > 0:
            conv = convs[(pair - 1) % 2]
            for head in range(PAIR // HEAD_DIM):
                columns = slice(head * HEAD_DIM, (head + 1) * HEAD_DIM)
                start = (pair - 1) * PAIR + head * HEAD_DIM
                result[:, start : start + HEAD_DIM] = attend(
                    conv[0, BACK:, columns], conv[1, :, columns], conv[2, :, columns], bias_ref[...]
                )
    copy = pltpu.make_async_copy(result, out_ref.at[pl.ds(0, BACK)], out_sem)
    copy.start()
    copy.wait()


VMEM = pl.BlockSpec(memory_space=pltpu.VMEM)
ANY = pl.BlockSpec(memory_space=pl.ANY)


def scratch(kinds, rows, queries):
    return [
        pltpu.VMEM((kinds, 8 + rows, PAIR), jnp.float32),
        pltpu.VMEM((kinds, 8 + rows, PAIR), jnp.float32),
        pltpu.VMEM((kinds, rows, PAIR), jnp.bfloat16),
        pltpu.VMEM((kinds, rows, PAIR), jnp.bfloat16),
        pltpu.VMEM((2, rows, LANES), jnp.float32),
        pltpu.VMEM((queries, rows), jnp.float32),
    ]


def main_part(rows, own, other, taps):
    frames = rows.shape[0]
    kinds, width, half = own.shape
    inner = 2 * half
    return pl.pallas_call(
        main_kernel,
        out_shape=(
            jax.ShapeDtypeStruct((frames, inner), jnp.bfloat16),
            jax.ShapeDtypeStruct((kinds, BACK, inner), jnp.float32),
        ),
        in_specs=[VMEM, VMEM, VMEM, VMEM, VMEM],
        out_specs=(VMEM, VMEM),
        scratch_shapes=scratch(kinds, frames, frames - BACK),
        compiler_params=pltpu.CompilerParams(vmem_limit_bytes=LIMIT),
        name="main_rows",
    )(rows, own, other, *taps)


def halo_part(halo, lag, own, other, taps, first, attended):
    kinds, width, half = own.shape
    inner = 2 * half
    return pl.pallas_call(
        halo_kernel,
        out_shape=jax.ShapeDtypeStruct(attended.shape, jnp.bfloat16),
        in_specs=[VMEM, VMEM, VMEM, VMEM, VMEM, VMEM, VMEM, ANY],
        out_specs=ANY,
        scratch_shapes=scratch(kinds, 2 * BACK, BACK)
        + [
            pltpu.VMEM((BACK, inner), jnp.bfloat16),
            pltpu.SemaphoreType.DMA,
        ],
        input_output_aliases={7: 0},
        compiler_params=pltpu.CompilerParams(vmem_limit_bytes=LIMIT),
        name="halo_rows",
    )(halo, lag, own, other, *taps, first, attended)


def shards(tokens, w_qkv, conv_taps, w_out, episode_start):
    frames, positions, model_width = tokens.shape
    inner_width = w_qkv.shape[2]
    share = positions // CORES
    core = lax.axis_index("core")
    device_row = lax.axis_index(("y", "z", "x"))
    out_half = model_width // CORES

    taps_other = lax.ppermute(conv_taps, "core", SWAP)
    tokens_f = lax.dynamic_slice_in_dim(tokens, core * share, share, 1).astype(jnp.float32)
    inv_rms = lax.rsqrt(jnp.mean(tokens_f * tokens_f, axis=-1, keepdims=True) + 1e-06)
    normed = (tokens_f * inv_rms).astype(jnp.bfloat16).transpose(1, 0, 2)
    frame_ids = device_row * frames + jnp.arange(frames, dtype=jnp.int32)
    lag = (frame_ids - episode_start).astype(jnp.bfloat16)
    packed = jnp.concatenate(
        [normed, jnp.broadcast_to(lag[None, :, None], (share, frames, LANES))], axis=2
    )
    packed, taps_other, w_sent = lax.optimization_barrier((packed, taps_other, w_qkv))
    w_other = lax.ppermute(w_sent, "core", SWAP)
    w_own = lax.ppermute(w_sent, "core", [(0, 0), (1, 1)])
    with jax.named_scope("gather"):
        rows = lax.all_to_all(packed, ("z", "x"), 0, 0, tiled=True)
    with jax.named_scope("theirs"):
        theirs = lax.dynamic_slice_in_dim(w_out, (1 - core) * out_half, out_half, 1)
    w_out_other = lax.ppermute(theirs, "core", SWAP)
    with jax.named_scope("mine"):
        mine = lax.dynamic_slice_in_dim(w_out, core * out_half, out_half, 1)
    rows = rows.reshape(GROUP * frames, model_width + LANES)
    halo = lax.ppermute(rows[-BACK:], "y", [(y, y + 1) for y in range(PLANES - 1)])

    taps = (conv_taps, taps_other)
    attended, first = main_part(rows, w_own, w_other, taps)
    attended = halo_part(
        halo, rows[:BACK, model_width:], w_own, w_other, taps, first, attended
    )
    with jax.named_scope("back"):
        back = lax.all_to_all(
            attended.reshape(GROUP, frames, CORES * inner_width), ("z", "x"), 0, 0, tiled=True
        )
    back_other = lax.ppermute(back, "core", SWAP)

    def output(part, first, second):
        flat = part.reshape(share * frames, CORES * inner_width)
        return (
            jnp.dot(flat[:, :inner_width], first, preferred_element_type=jnp.float32)
            + jnp.dot(flat[:, inner_width:], second, preferred_element_type=jnp.float32)
        ).astype(jnp.bfloat16).reshape(share, frames, out_half).transpose(1, 0, 2)

    out_mine = output(back, mine, w_out_other)
    out_other = output(back_other, w_out_other, mine)
    result = jnp.zeros((frames, positions, out_half), jnp.bfloat16)
    result = lax.dynamic_update_slice_in_dim(result, out_mine, core * share, 1)
    return lax.dynamic_update_slice_in_dim(result, out_other, (1 - core) * share, 1)


def solution(mesh):
    grid = Mesh(mesh.devices.reshape(PLANES, ROWS, COLS, CORES), ("y", "z", "x", "core"))
    seq = ("y", "z", "x")
    in_specs = (
        P(seq, None, None),
        P(None, None, "core"),
        P(None, None, "core"),
        P("core", None),
        P(seq),
    )
    return jax.shard_map(
        shards, mesh=grid, in_specs=in_specs, out_specs=P(seq, None, "core"), check_vma=False
    )
```

time: 106 us -> 92.3 us (0.87)
  blocking collectives: 0 us -> 39.7 us
  waiting for transfers between devices: 38.7 us -> 11.1 us
  matrix products: 22 us -> 3.66 us
  starting transfers between devices: 28.5 us -> 20.9 us
  Pallas kernels: 8.53 us -> 10.9 us
  other arithmetic: 3.7 us -> 1.44 us
    all_to_all x0 -> x1, blocking collectives: none -> 39.7 us  [shards(): rows = lax.all_to_all(packed, ('z', 'x'), 0, 0, tiled=True)]
    all_to_all x1 -> x0, waiting for transfers between devices: 26.4 us -> none  [shards(): rows = lax.all_to_all(packed, ('z', 'x'), 0, 0, tiled=True)]
    dot_general x4 -> x0, matrix products: 18.4 us -> none  [project(): jnp.einsum('nd,cde->cne', part[:, :model_width], weight, preferred_elemen...]
    all_to_all x1 -> x0, starting transfers between devices: 9.33 us -> none  [shards(): rows = lax.all_to_all(packed, ('z', 'x'), 0, 0, tiled=True)]
    ppermute x1, starting transfers between devices: 0.54 us -> 3.2 us  [shards(): taps_other = lax.ppermute(conv_taps, 'core', SWAP)]
    pallas_call x1 -> x2, Pallas kernels: 8.53 us -> 10.9 us  [the longest x1 6.05 us: main_part(): pl.pallas_call(main_kernel, out_shape=(jax.ShapeDtypeStruct((frames, inne...]
    ppermute x1 -> x2, starting transfers between devices: 3.2 us -> 2.94 us  [the longest x1 2.79 us: shards(): w_own = lax.ppermute(w_sent, 'core', [(0, 0), (1, 1)])]
  transfers between devices with their start and end apart: 7 -> 7, of which waited for: 3 -> 1; matrix products, arithmetic and copies ran while one was open for 16% -> 8% of each run, Pallas kernels for 0% -> 7%
where the time goes in v2:
time: 92.3 us; the launch traced here: 92 us
  blocking collectives  39.7 us (43%)
  starting transfers between devices  20.9 us (23%)
  waiting for transfers between devices  11.1 us (12%)
  Pallas kernels  10.9 us (12%)
  local copies, waits for them, and re-layouts  4.09 us (4%)
  matrix products  3.66 us (4%)
  other arithmetic  1.44 us (2%)
    all_to_all x1, blocking collectives, shards(): rows = lax.all_to_all(packed, ('z', 'x'), 0, 0, tiled=True)  39.7 us
    all_to_all x1, waiting for transfers between devices, shards(): lax.all_to_all(attended.reshape(GROUP, frames, CORES * inner_width), ('z'...  11.1 us
    pallas_call x1, Pallas kernels, main_part(): pl.pallas_call(main_kernel, out_shape=(jax.ShapeDtypeStruct((frames, inne...  6.05 us
    pallas_call x1, Pallas kernels, halo_part(): pl.pallas_call(halo_kernel, out_shape=jax.ShapeDtypeStruct(attended.shape...  4.86 us
    all_to_all x1, starting transfers between devices, shards(): lax.all_to_all(attended.reshape(GROUP, frames, CORES * inner_width), ('z'...  4.64 us
    ppermute x1, starting transfers between devices, shards(): back_other = lax.ppermute(back, 'core', SWAP)  4.54 us
    ppermute x1, starting transfers between devices, shards(): lax.ppermute(rows[-BACK:], 'y', [(y, y + 1) for y in range(PLANES - 1)])  3.22 us
    ppermute x1, starting transfers between devices, shards(): taps_other = lax.ppermute(conv_taps, 'core', SWAP)  3.2 us
  transfers between devices with their start and end apart: 7, of which 1 were waited for; matrix products, arithmetic and copies ran while one was open for 8% of the time, Pallas kernels for 7%

profile of v2, /device:TPU:1, one launch (start us, length us, event | category | flops | bytes accessed | tf_op | source)
XLA Modules:
  0.0 92.0 jit_solution(11670859981287422337)
XLA Ops:
  0.0 0.0 copy-start
  0.0 3.2 %collective-permute-start = (f32[3,3,512]{2,1,0:T(4,128)}, f32[3,3,512]{2,1,0:T(4,128)S(1)}, u32[]{:S(2)}, u32[]{:S(2)}) collective-permute-start(f32[3,3,512]{2,1,0:T(4,128)} %taps_own.3), channel_id=1, source_target_pairs={{0,1},{1,0},{2,3},{3,2},{4,5},{5,4},{6,7},{7,6},{8,9},{9,8},{10,11... | collective-permute-start | bytes 55304 | tf_op jit(solution)/shard_map/ppermute | solution.py:195
  3.2 1.3 %constant_dynamic-slice_fusion.1 = bf16[8,32,2048]{2,1,0:T(8,128)(2,1)S(1)} fusion(bf16[8,64,2048]{2,1,0:T(8,128)(2,1)} %param.5, s32[]{:T(128)S(6)} %select_n.13), kind=kLoop, calls=%fused_computation.27 | loop fusion | bytes 2097156 | tf_op jit(solution)/shard_map/dynamic_slice | solution.py:196
  4.5 0.0 copy-start.3
  4.5 0.7 fusion
  5.3 0.6 fusion.6
  5.9 0.0 copy-done.3
  5.9 0.1 broadcast_in_dim.5
  6.0 0.0 copy-start.1
  6.0 0.1 pad_maximum_fusion
  6.1 0.0 collective-permute-done.taps_other
  6.1 2.8 %collective-permute-start.2 = (bf16[3,2048,512]{2,1,0:T(8,128)(2,1)}, bf16[3,2048,512]{2,1,0:T(8,128)(2,1)S(1)}, u32[]{:S(2)}, u32[]{:S(2)}) collective-permute-start(bf16[3,2048,512]{2,1,0:T(8,128)(2,1)} %param.6), channel_id=1, source_target_pairs={{0,0},{1,1},{2,2},{3,3},{4,4},{5,5},{6,6},{7,7},{8,8},{9,9},{10,10... | collective-permute-start | bytes 18874376 | tf_op jit(solution)/shard_map/ppermute | solution.py:206
  8.9 0.2 collective-permute-start.3
  9.1 39.7 %all_to_all.10 = bf16[32,8,2176]{2,1,0:T(8,128)(2,1)S(1)} all-to-all(bf16[32,8,2176]{2,1,0:T(8,128)(2,1)S(1)} %pad_maximum_fusion), channel_id=1, replica_groups=mesh['y'=4,'z'=8,'x'=4,'core'=2] {'z','x'}, dimensions={0} | all-to-all | bytes 2228224 | tf_op jit(solution)/shard_map/gather/all_to_all | solution.py:208
  48.8 3.2 %collective-permute-start.1 = (bf16[64,2176]{1,0:T(8,128)(2,1)S(1)}, bf16[64,2176]{1,0:T(8,128)(2,1)S(1)}, u32[]{:S(2)}, u32[]{:S(2)}) collective-permute-start(bf16[64,2176]{1,0:T(8,128)(2,1)S(1)} %slice_bitcast_fusion), channel_id=1, source_target_pairs={{0,64},{64,128},{128,192},{1,65},{65,129},{129,193},{2,66},{66,130... | collective-permute-start | bytes 835592 | tf_op jit(solution)/shard_map/ppermute | solution.py:215
  52.0 0.0 collective-permute-done.2.own
  52.0 0.0 collective-permute-done.3.other
  52.0 0.0 copy-done.1
  52.1 6.0 %main_rows.1 = (bf16[256,1024]{1,0:T(8,128)(2,1)}, f32[3,64,1024]{2,1,0:T(8,128)S(1)}) custom-call(bf16[256,2176]{1,0:T(8,128)(2,1)S(1)} %bitcast.19, bf16[3,2048,512]{2,1,0:T(8,128)(2,1)S(1)} %collective-permute-done.2.own, bf16[3,2048,512]{2,1,0:T(8,128)(2,1)S(1)} %collective-permute-done.3.other, f32[3,3,512]{2,1,0:T(4,128)S(1)} %copy-done.1, ...), custom_call_target="tpu_custom_call" | custom-call | tf_op jit(solution)/shard_map/main_rows/pallas_call | solution.py:154
  58.1 0.0 collective-permute-done.1.x_ref
  58.1 4.9 %halo_rows.1 = bf16[256,1024]{1,0:T(8,128)(2,1)} custom-call(bf16[64,2176]{1,0:T(8,128)(2,1)S(1)} %collective-permute-done.1.x_ref, bf16[64,128]{1,0:T(8,128)(2,1)S(1)} %slice.29.lag_ref, bf16[3,2048,512]{2,1,0:T(8,128)(2,1)S(1)} %collective-permute-done.2.own, ...), custom_call_target="tpu_custom_call", output_to_operand_aliasing={{}: (7, {})} | custom-call | tf_op jit(solution)/shard_map/halo_rows/pallas_call | solution.py:171
  63.0 4.6 %all-to-all-start.1 = ((bf16[32,8,1024]{2,1,0:T(8,128)(2,1)}), bf16[32,8,1024]{2,1,0:T(8,128)(2,1)}, u32[]{:S(2)}, u32[]{:S(2)}) async-start(bf16[32,8,1024]{2,1,0:T(8,128)(2,1)} %bitcast.3), calls=%async_computation.1 | async-start | bytes 1048576 | tf_op jit(solution)/shard_map/back/all_to_all | solution.py:223
  67.6 0.0 copy-done
  67.6 1.1 %constant_dynamic-slice_fusion = bf16[512,1024]{1,0:T(8,128)(2,1)} fusion(bf16[512,2048]{1,0:T(8,128)(2,1)S(1)} %copy-done, s32[]{:T(128)S(6)} %select_n.15), kind=kLoop, calls=%fused_computation.25 | loop fusion | bytes 2097156 | tf_op jit(solution)/shard_map/theirs/dynamic_slice | solution.py:210
  68.7 2.4 %collective-permute-start.4 = (bf16[512,1024]{1,0:T(8,128)(2,1)}, bf16[512,1024]{1,0:T(8,128)(2,1)S(1)}, u32[]{:S(2)}, u32[]{:S(2)}) collective-permute-start(bf16[512,1024]{1,0:T(8,128)(2,1)} %constant_dynamic-slice_fusion), channel_id=1, source_target_pairs={{0,1},{1,0},{2,3},{3,2},{4,5},{5,4},{6,7},{7,6},{8,9},{9,8},{10,11... | collective-permute-start | bytes 3145736 | tf_op jit(solution)/shard_map/ppermute | solution.py:211
  71.1 11.1 %all-to-all-done.1 = bf16[32,8,1024]{2,1,0:T(8,128)(2,1)} async-done(((bf16[32,8,1024]{2,1,0:T(8,128)(2,1)}), bf16[32,8,1024]{2,1,0:T(8,128)(2,1)}, u32[]{:S(2)}, u32[]{:S(2)}) %all-to-all-start.1) | async-done | bytes 524320 | tf_op jit(solution)/shard_map/back/all_to_all | solution.py:223
  82.2 4.5 %collective-permute-start.5 = (bf16[32,8,1024]{2,1,0:T(8,128)(2,1)}, bf16[32,8,1024]{2,1,0:T(8,128)(2,1)S(1)}, u32[]{:S(2)}, u32[]{:S(2)}) collective-permute-start(bf16[32,8,1024]{2,1,0:T(8,128)(2,1)} %all-to-all-done.1), channel_id=1, source_target_pairs={{0,1},{1,0},{2,3},{3,2},{4,5},{5,4},{6,7},{7,6},{8,9},{9,8},{10,11... | collective-permute-start | bytes 1572872 | tf_op jit(solution)/shard_map/ppermute | solution.py:226
  86.7 1.4 %fusion.9 = f32[256,1024]{1,0:T(8,128)S(1)} fusion(bf16[512,2048]{1,0:T(8,128)(2,1)S(1)} %copy-done, s32[]{:T(128)S(6)} %select_n.14, bf16[256,1024]{1,0:T(8,128)(2,1)} %bitcast.4), kind=kOutput, calls=%fused_computation.14 | convolution fusion | flops 268435456 | bytes 2359300 | tf_op jit(solution)/shard_map/dot_general | solution.py:231
  88.1 0.0 collective-permute-done.4
  88.1 1.4 %fusion.5 = bf16[32,8,1024]{2,1,0:T(8,128)(2,1)S(1)} fusion(f32[256,1024]{1,0:T(8,128)S(1)} %fusion.9, bf16[512,1024]{1,0:T(8,128)(2,1)S(1)} %collective-permute-done.4, bf16[256,1024]{1,0:T(8,128)(2,1)} %bitcast.4), kind=kOutput, calls=%fused_computation.9 | convolution fusion | flops 268959744 | bytes 2883584 | tf_op jit(solution)/shard_map/dot_general | solution.py:232
  89.5 0.1 broadcast_in_dim.4
  89.6 0.3 bitcast_dynamic-update-slice_fusion.1
  90.0 0.0 copy-start.2
  90.0 0.0 collective-permute-done.5
  90.0 0.4 fusion.7
  90.4 0.4 fusion.4
  90.9 0.0 copy-done.2
  90.9 1.1 %bitcast_dynamic-update-slice_fusion = bf16[8,64,1024]{2,1,0:T(8,128)(2,1)} fusion(bf16[8,64,1024]{2,1,0:T(8,128)(2,1)} %copy-done.2, s32[]{:T(128)S(6)} %select_n.16, bf16[32,8,1024]{2,1,0:T(8,128)(2,1)S(1)} %fusion.4), kind=kLoop, calls=%fused_computation.16 | loop fusion | bytes 1048580 | tf_op jit(solution)/shard_map/dynamic_update_slice | solution.py:239
  (4 shorter events, 0.0 us)
Async XLA Ops:
  0.0 67.6 %copy-start = (bf16[512,2048]{1,0:T(8,128)(2,1)S(1)}, bf16[512,2048]{1,0:T(8,128)(2,1)}, u32[]{:S(2)}) copy-start(bf16[512,2048]{1,0:T(8,128)(2,1)} %param.8) | copy-start | bytes 6291460
  0.0 6.1 %collective-permute-start = (f32[3,3,512]{2,1,0:T(4,128)}, f32[3,3,512]{2,1,0:T(4,128)S(1)}, u32[]{:S(2)}, u32[]{:S(2)}) collective-permute-start(f32[3,3,512]{2,1,0:T(4,128)} %taps_own.3), channel_id=1, source_target_pairs={{0,1},{1,0},{2,3},{3,2},{4,5},{5,4},{6,7},{7,6},{8,9},{9,8},{10,11... | collective-permute-start | bytes 55304 | tf_op jit(solution)/shard_map/ppermute | solution.py:195
  4.5 1.4 %copy-start.3 = (s32[8]{0:T(128)S(1)}, s32[8]{0:T(128)}, u32[]{:S(2)}) copy-start(s32[8]{0:T(128)} %param.9) | copy-start | bytes 100
  6.0 46.1 %copy-start.1 = (f32[3,3,512]{2,1,0:T(4,128)S(1)}, f32[3,3,512]{2,1,0:T(4,128)}, u32[]{:S(2)}) copy-start(f32[3,3,512]{2,1,0:T(4,128)} %taps_own.3) | copy-start | bytes 55300
  6.1 45.9 %collective-permute-start.2 = (bf16[3,2048,512]{2,1,0:T(8,128)(2,1)}, bf16[3,2048,512]{2,1,0:T(8,128)(2,1)S(1)}, u32[]{:S(2)}, u32[]{:S(2)}) collective-permute-start(bf16[3,2048,512]{2,1,0:T(8,128)(2,1)} %param.6), channel_id=1, source_target_pairs={{0,0},{1,1},{2,2},{3,3},{4,4},{5,5},{6,6},{7,7},{8,8},{9,9},{10,10... | collective-permute-start | bytes 18874376 | tf_op jit(solution)/shard_map/ppermute | solution.py:206
  8.9 43.1 %collective-permute-start.3 = (bf16[3,2048,512]{2,1,0:T(8,128)(2,1)}, bf16[3,2048,512]{2,1,0:T(8,128)(2,1)S(1)}, u32[]{:S(2)}, u32[]{:S(2)}) collective-permute-start(bf16[3,2048,512]{2,1,0:T(8,128)(2,1)} %param.6), channel_id=1, source_target_pairs={{0,1},{1,0},{2,3},{3,2},{4,5},{5,4},{6,7},{7,6},{8,9},{9,8},{10,11... | collective-permute-start | bytes 18874376 | tf_op jit(solution)/shard_map/ppermute | solution.py:205
  48.8 9.3 %collective-permute-start.1 = (bf16[64,2176]{1,0:T(8,128)(2,1)S(1)}, bf16[64,2176]{1,0:T(8,128)(2,1)S(1)}, u32[]{:S(2)}, u32[]{:S(2)}) collective-permute-start(bf16[64,2176]{1,0:T(8,128)(2,1)S(1)} %slice_bitcast_fusion), channel_id=1, source_target_pairs={{0,64},{64,128},{128,192},{1,65},{65,129},{129,193},{2,66},{66,130... | collective-permute-start | bytes 835592 | tf_op jit(solution)/shard_map/ppermute | solution.py:215
  63.0 19.2 %all-to-all-start.1 = ((bf16[32,8,1024]{2,1,0:T(8,128)(2,1)}), bf16[32,8,1024]{2,1,0:T(8,128)(2,1)}, u32[]{:S(2)}, u32[]{:S(2)}) async-start(bf16[32,8,1024]{2,1,0:T(8,128)(2,1)} %bitcast.3), calls=%async_computation.1 | async-start | bytes 1048576 | tf_op jit(solution)/shard_map/back/all_to_all | solution.py:223
  68.7 19.4 %collective-permute-start.4 = (bf16[512,1024]{1,0:T(8,128)(2,1)}, bf16[512,1024]{1,0:T(8,128)(2,1)S(1)}, u32[]{:S(2)}, u32[]{:S(2)}) collective-permute-start(bf16[512,1024]{1,0:T(8,128)(2,1)} %constant_dynamic-slice_fusion), channel_id=1, source_target_pairs={{0,1},{1,0},{2,3},{3,2},{4,5},{5,4},{6,7},{7,6},{8,9},{9,8},{10,11... | collective-permute-start | bytes 3145736 | tf_op jit(solution)/shard_map/ppermute | solution.py:211
  82.2 7.8 %collective-permute-start.5 = (bf16[32,8,1024]{2,1,0:T(8,128)(2,1)}, bf16[32,8,1024]{2,1,0:T(8,128)(2,1)S(1)}, u32[]{:S(2)}, u32[]{:S(2)}) collective-permute-start(bf16[32,8,1024]{2,1,0:T(8,128)(2,1)} %all-to-all-done.1), channel_id=1, source_target_pairs={{0,1},{1,0},{2,3},{3,2},{4,5},{5,4},{6,7},{7,6},{8,9},{9,8},{10,11... | collective-permute-start | bytes 1572872 | tf_op jit(solution)/shard_map/ppermute | solution.py:226
  90.0 1.0 %copy-start.2 = (bf16[8,64,1024]{2,1,0:T(8,128)(2,1)}, bf16[8,64,1024]{2,1,0:T(8,128)(2,1)S(1)}, u32[]{:S(2)}) copy-start(bf16[8,64,1024]{2,1,0:T(8,128)(2,1)S(1)} %bitcast_dynamic-update-slice_fusion.1) | copy-start | bytes 3145732

commit v3 on v2

--- a/solution.py
+++ b/solution.py
@@ -15,7 +15,8 @@
 GROUP = ROWS * COLS
 LANES = 128
 PAIR = 256
-LIMIT = 12 * 1024 * 1024
+LIMIT = 38 * 1024 * 1024
+HALO_LIMIT = 16 * 1024 * 1024
 SWAP = [(0, 1), (1, 0)]
 
 
@@ -50,22 +51,34 @@
     return jnp.where((age >= 0) & (age <= query_lag), 0.0, -1e30)
 
 
-def weight_of(own, other, pair, kind):
-    per_side = own.shape[2] // PAIR
-    side = own if pair < per_side else other
+def fetch(streamed, buffer, sems):
+    copies = []
+    for kind in range(streamed.shape[0]):
+        copies.append(pltpu.make_async_copy(streamed.at[kind], buffer.at[kind], sems.at[kind]))
+        copies[-1].start()
+    return copies
+
+
+def weight_of(resident, buffer, copies, pair, kind):
+    per_side = resident.shape[2] // PAIR
     first = (pair % per_side) * PAIR
-    return side[kind, :, first : first + PAIR]
-
-
-def main_kernel(x_ref, own, other, taps_own, taps_other, out_ref, first_ref, pad0, pad1, conv0, conv1, mask_ref, bias_ref):
+    if pair < per_side:
+        return resident[kind, :, first : first + PAIR]
+    if pair == per_side and copies is not None:
+        copies[kind].wait()
+    return buffer[kind, :, first : first + PAIR]
+
+
+def main_kernel(x_ref, resident, streamed, taps_first, taps_second, out_ref, first_ref, buffer, pad0, pad1, conv0, conv1, mask_ref, bias_ref, sems):
     frames = x_ref.shape[0]
-    width = own.shape[1]
-    per_side = own.shape[2] // PAIR
+    width = resident.shape[1]
+    per_side = resident.shape[2] // PAIR
+    copies = fetch(streamed, buffer, sems)
     lag = x_ref[:, width : width + LANES].astype(jnp.float32)
     for step in (1, 2):
         mask_ref[step - 1] = (lag >= step).astype(jnp.float32)
     bias_ref[...] = mask_bias(lag[BACK:, 0:1], BACK, frames - BACK, frames)
-    pads, convs, taps = (pad0, pad1), (conv0, conv1), (taps_own, taps_other)
+    pads, convs, taps = (pad0, pad1), (conv0, conv1), (taps_first, taps_second)
     for pad in pads:
         for kind in range(3):
             pad[kind, 0:8] = jnp.zeros((8, PAIR), jnp.float32)
@@ -74,7 +87,7 @@
             pad, conv = pads[pair % 2], convs[pair % 2]
             for kind in range(3):
                 projected = jnp.dot(
-                    x_ref[:, :width], weight_of(own, other, pair, kind), preferred_element_type=jnp.float32
+                    x_ref[:, :width], weight_of(resident, buffer, copies, pair, kind), preferred_element_type=jnp.float32
                 )
                 pad[kind, 8 : 8 + frames] = projected
                 first_ref[kind, :, pair * PAIR : (pair + 1) * PAIR] = projected[:BACK]
@@ -92,18 +105,18 @@
                 )
 
 
-def halo_kernel(x_ref, lag_ref, own, other, taps_own, taps_other, first_ref, done_ref, out_ref, pad0, pad1, conv0, conv1, mask_ref, bias_ref, result, out_sem):
+def halo_kernel(x_ref, lag_ref, resident, buffer, taps_first, taps_second, first_ref, done_ref, out_ref, pad0, pad1, conv0, conv1, mask_ref, bias_ref, result, out_sem):
     del done_ref
     rows = 2 * BACK
-    width = own.shape[1]
-    per_side = own.shape[2] // PAIR
+    width = resident.shape[1]
+    per_side = resident.shape[2] // PAIR
     halo_lag = x_ref[:, width : width + LANES].astype(jnp.float32)
     lag = lag_ref[...].astype(jnp.float32)
     for step in (1, 2):
         mask_ref[step - 1, :BACK] = (halo_lag >= step).astype(jnp.float32)
         mask_ref[step - 1, BACK:] = (lag >= step).astype(jnp.float32)
     bias_ref[...] = mask_bias(lag[:, 0:1], BACK, BACK, rows)
-    pads, convs, taps = (pad0, pad1), (conv0, conv1), (taps_own, taps_other)
+    pads, convs, taps = (pad0, pad1), (conv0, conv1), (taps_first, taps_second)
     for pad in pads:
         for kind in range(3):
             pad[kind, 0:8] = jnp.zeros((8, PAIR), jnp.float32)
@@ -112,7 +125,7 @@
             pad, conv = pads[pair % 2], convs[pair % 2]
             for kind in range(3):
                 pad[kind, 8 : 8 + BACK] = jnp.dot(
-                    x_ref[:, :width], weight_of(own, other, pair, kind), preferred_element_type=jnp.float32
+                    x_ref[:, :width], weight_of(resident, buffer, None, pair, kind), preferred_element_type=jnp.float32
                 )
                 pad[kind, 8 + BACK : 8 + rows] = first_ref[kind, :, pair * PAIR : (pair + 1) * PAIR]
                 convolve(
@@ -147,31 +160,33 @@
     ]
 
 
-def main_part(rows, own, other, taps):
+def main_part(rows, resident, streamed, taps):
     frames = rows.shape[0]
-    kinds, width, half = own.shape
+    kinds, width, half = resident.shape
     inner = 2 * half
     return pl.pallas_call(
         main_kernel,
         out_shape=(
             jax.ShapeDtypeStruct((frames, inner), jnp.bfloat16),
             jax.ShapeDtypeStruct((kinds, BACK, inner), jnp.float32),
+            jax.ShapeDtypeStruct(streamed.shape, streamed.dtype),
         ),
-        in_specs=[VMEM, VMEM, VMEM, VMEM, VMEM],
-        out_specs=(VMEM, VMEM),
-        scratch_shapes=scratch(kinds, frames, frames - BACK),
+        in_specs=[VMEM, VMEM, ANY, VMEM, VMEM],
+        out_specs=(VMEM, VMEM, VMEM),
+        scratch_shapes=scratch(kinds, frames, frames - BACK)
+        + [pltpu.SemaphoreType.DMA((kinds,))],
         compiler_params=pltpu.CompilerParams(vmem_limit_bytes=LIMIT),
         name="main_rows",
-    )(rows, own, other, *taps)
-
-
-def halo_part(halo, lag, own, other, taps, first, attended):
-    kinds, width, half = own.shape
+    )(rows, resident, streamed, *taps)
+
+
+def halo_part(halo, lag, resident, streamed, taps, first, attended):
+    kinds, width, half = resident.shape
     inner = 2 * half
     return pl.pallas_call(
         halo_kernel,
         out_shape=jax.ShapeDtypeStruct(attended.shape, jnp.bfloat16),
-        in_specs=[VMEM, VMEM, VMEM, VMEM, VMEM, VMEM, VMEM, ANY],
+        in_specs=[VMEM] * 7 + [ANY],
         out_specs=ANY,
         scratch_shapes=scratch(kinds, 2 * BACK, BACK)
         + [
@@ -179,9 +194,9 @@
             pltpu.SemaphoreType.DMA,
         ],
         input_output_aliases={7: 0},
-        compiler_params=pltpu.CompilerParams(vmem_limit_bytes=LIMIT),
+        compiler_params=pltpu.CompilerParams(vmem_limit_bytes=HALO_LIMIT),
         name="halo_rows",
-    )(halo, lag, own, other, *taps, first, attended)
+    )(halo, lag, resident, streamed, *taps, first, attended)
 
 
 def shards(tokens, w_qkv, conv_taps, w_out, episode_start):
@@ -203,7 +218,6 @@
     )
     packed, taps_other, w_sent = lax.optimization_barrier((packed, taps_other, w_qkv))
     w_other = lax.ppermute(w_sent, "core", SWAP)
-    w_own = lax.ppermute(w_sent, "core", [(0, 0), (1, 1)])
     with jax.named_scope("gather"):
         rows = lax.all_to_all(packed, ("z", "x"), 0, 0, tiled=True)
     with jax.named_scope("theirs"):
@@ -214,10 +228,10 @@
     rows = rows.reshape(GROUP * frames, model_width + LANES)
     halo = lax.ppermute(rows[-BACK:], "y", [(y, y + 1) for y in range(PLANES - 1)])
 
-    taps = (conv_taps, taps_other)
-    attended, first = main_part(rows, w_own, w_other, taps)
+    taps = (taps_other, conv_taps)
+    attended, first, loaded = main_part(rows, w_other, w_qkv, taps)
     attended = halo_part(
-        halo, rows[:BACK, model_width:], w_own, w_other, taps, first, attended
+        halo, rows[:BACK, model_width:], w_other, loaded, taps, first, attended
     )
     with jax.named_scope("back"):
         back = lax.all_to_all(
@@ -232,8 +246,8 @@
             + jnp.dot(flat[:, inner_width:], second, preferred_element_type=jnp.float32)
         ).astype(jnp.bfloat16).reshape(share, frames, out_half).transpose(1, 0, 2)
 
-    out_mine = output(back, mine, w_out_other)
-    out_other = output(back_other, w_out_other, mine)
+    out_mine = output(back, w_out_other, mine)
+    out_other = output(back_other, mine, w_out_other)
     result = jnp.zeros((frames, positions, out_half), jnp.bfloat16)
     result = lax.dynamic_update_slice_in_dim(result, out_mine, core * share, 1)
     return lax.dynamic_update_slice_in_dim(result, out_other, (1 - core) * share, 1)

time: 92.3 us -> 91 us (0.986)
  starting transfers between devices: 20.9 us -> 18.2 us
  Pallas kernels: 10.9 us -> 12.3 us
    ppermute x1 -> x0, starting transfers between devices: 2.79 us -> none  [shards(): w_own = lax.ppermute(w_sent, 'core', [(0, 0), (1, 1)])]
    pallas_call x1, Pallas kernels: 6.05 us -> 7.54 us  [main_part(): pl.pallas_call(main_kernel, out_shape=(jax.ShapeDtypeStruct((frames, inne...]
  transfers between devices with their start and end apart: 7 -> 6, of which waited for: 1 -> 1; matrix products, arithmetic and copies ran while one was open for 8% -> 8% of each run, Pallas kernels for 7% -> 8%
where the time goes in v3:
time: 91 us; the launch traced here: 90.7 us
  blocking collectives  39.7 us (44%)
  starting transfers between devices  18.2 us (20%)
  Pallas kernels  12.3 us (14%)
  waiting for transfers between devices  11.1 us (12%)
  local copies, waits for them, and re-layouts  4.09 us (4%)
  matrix products  3.66 us (4%)
  other arithmetic  1.44 us (2%)
    all_to_all x1, blocking collectives, shards(): rows = lax.all_to_all(packed, ('z', 'x'), 0, 0, tiled=True)  39.7 us
    all_to_all x1, waiting for transfers between devices, shards(): lax.all_to_all(attended.reshape(GROUP, frames, CORES * inner_width), ('z'...  11.1 us
    pallas_call x1, Pallas kernels, main_part(): pl.pallas_call(main_kernel, out_shape=(jax.ShapeDtypeStruct((frames, inne...  7.54 us
    pallas_call x1, Pallas kernels, halo_part(): pl.pallas_call(halo_kernel, out_shape=jax.ShapeDtypeStruct(attended.shape...  4.78 us
    all_to_all x1, starting transfers between devices, shards(): lax.all_to_all(attended.reshape(GROUP, frames, CORES * inner_width), ('z'...  4.63 us
    ppermute x1, starting transfers between devices, shards(): back_other = lax.ppermute(back, 'core', SWAP)  4.54 us
    ppermute x1, starting transfers between devices, shards(): lax.ppermute(rows[-BACK:], 'y', [(y, y + 1) for y in range(PLANES - 1)])  3.22 us
    ppermute x1, starting transfers between devices, shards(): taps_other = lax.ppermute(conv_taps, 'core', SWAP)  3.2 us
  transfers between devices with their start and end apart: 6, of which 1 were waited for; matrix products, arithmetic and copies ran while one was open for 8% of the time, Pallas kernels for 8%

profile of v3, /device:TPU:1, one launch (start us, length us, event | category | flops | bytes accessed | tf_op | source)
XLA Modules:
  0.0 90.7 jit_solution(8620381455245258680)
XLA Ops:
  0.0 0.0 copy-start
  0.0 3.2 %collective-permute-start = (f32[3,3,512]{2,1,0:T(4,128)}, f32[3,3,512]{2,1,0:T(4,128)S(1)}, u32[]{:S(2)}, u32[]{:S(2)}) collective-permute-start(f32[3,3,512]{2,1,0:T(4,128)} %taps_second.3), channel_id=1, source_target_pairs={{0,1},{1,0},{2,3},{3,2},{4,5},{5,4},{6,7},{7,6},{8,9},{9,8},{10,11... | collective-permute-start | bytes 55304 | tf_op jit(solution)/shard_map/ppermute | solution.py:210
  3.2 1.3 %constant_dynamic-slice_fusion.1 = bf16[8,32,2048]{2,1,0:T(8,128)(2,1)S(1)} fusion(bf16[8,64,2048]{2,1,0:T(8,128)(2,1)} %param.5, s32[]{:T(128)S(6)} %select_n.13), kind=kLoop, calls=%fused_computation.27 | loop fusion | bytes 2097156 | tf_op jit(solution)/shard_map/dynamic_slice | solution.py:211
  4.5 0.0 copy-start.3
  4.5 0.7 fusion
  5.3 0.6 fusion.6
  5.9 0.0 copy-done.3
  5.9 0.1 broadcast_in_dim.5
  6.0 0.0 copy-start.1
  6.0 0.1 pad_maximum_fusion
  6.1 0.0 collective-permute-done.taps_first
  6.1 0.2 collective-permute-start.2
  6.3 39.7 %all_to_all.10 = bf16[32,8,2176]{2,1,0:T(8,128)(2,1)S(1)} all-to-all(bf16[32,8,2176]{2,1,0:T(8,128)(2,1)S(1)} %pad_maximum_fusion), channel_id=1, replica_groups=mesh['y'=4,'z'=8,'x'=4,'core'=2] {'z','x'}, dimensions={0} | all-to-all | bytes 2228224 | tf_op jit(solution)/shard_map/gather/all_to_all | solution.py:222
  46.1 3.2 %collective-permute-start.1 = (bf16[64,2176]{1,0:T(8,128)(2,1)S(1)}, bf16[64,2176]{1,0:T(8,128)(2,1)S(1)}, u32[]{:S(2)}, u32[]{:S(2)}) collective-permute-start(bf16[64,2176]{1,0:T(8,128)(2,1)S(1)} %slice_bitcast_fusion), channel_id=1, source_target_pairs={{0,64},{64,128},{128,192},{1,65},{65,129},{129,193},{2,66},{66,130... | collective-permute-start | bytes 835592 | tf_op jit(solution)/shard_map/ppermute | solution.py:229
  49.3 0.0 collective-permute-done.2.resident
  49.3 0.0 copy-done.1
  49.3 7.5 %main_rows.1 = (bf16[256,1024]{1,0:T(8,128)(2,1)}, f32[3,64,1024]{2,1,0:T(8,128)S(1)}, bf16[3,2048,512]{2,1,0:T(8,128)(2,1)S(1)}) custom-call(bf16[256,2176]{1,0:T(8,128)(2,1)S(1)} %bitcast.19, bf16[3,2048,512]{2,1,0:T(8,128)(2,1)S(1)} %collective-permute-done.2.resident, bf16[3,2048,512]{2,1,0:T(8,128)(2,1)} %streamed.1, ...), custom_call_target="tpu_custom_call" | custom-call | tf_op jit(solution)/shard_map/main_rows/pallas_call | solution.py:167
  56.9 0.0 collective-permute-done.1.x_ref
  56.9 4.8 %halo_rows.1 = bf16[256,1024]{1,0:T(8,128)(2,1)} custom-call(bf16[64,2176]{1,0:T(8,128)(2,1)S(1)} %collective-permute-done.1.x_ref, bf16[64,128]{1,0:T(8,128)(2,1)S(1)} %slice.29.lag_ref, bf16[3,2048,512]{2,1,0:T(8,128)(2,1)S(1)} %collective-permute-done.2.resident, ...), custom_call_target="tpu_custom_call", output_to_operand_aliasing={{}: (7, {})} | custom-call | tf_op jit(solution)/shard_map/halo_rows/pallas_call | solution.py:186
  61.7 4.6 %all-to-all-start.1 = ((bf16[32,8,1024]{2,1,0:T(8,128)(2,1)}), bf16[32,8,1024]{2,1,0:T(8,128)(2,1)}, u32[]{:S(2)}, u32[]{:S(2)}) async-start(bf16[32,8,1024]{2,1,0:T(8,128)(2,1)} %bitcast.3), calls=%async_computation.1 | async-start | bytes 1048576 | tf_op jit(solution)/shard_map/back/all_to_all | solution.py:237
  66.3 0.0 copy-done
  66.3 1.1 %constant_dynamic-slice_fusion = bf16[512,1024]{1,0:T(8,128)(2,1)} fusion(bf16[512,2048]{1,0:T(8,128)(2,1)S(1)} %copy-done, s32[]{:T(128)S(6)} %select_n.14), kind=kLoop, calls=%fused_computation.26 | loop fusion | bytes 2097156 | tf_op jit(solution)/shard_map/theirs/dynamic_slice | solution.py:224
  67.4 2.4 %collective-permute-start.3 = (bf16[512,1024]{1,0:T(8,128)(2,1)}, bf16[512,1024]{1,0:T(8,128)(2,1)S(1)}, u32[]{:S(2)}, u32[]{:S(2)}) collective-permute-start(bf16[512,1024]{1,0:T(8,128)(2,1)} %constant_dynamic-slice_fusion), channel_id=1, source_target_pairs={{0,1},{1,0},{2,3},{3,2},{4,5},{5,4},{6,7},{7,6},{8,9},{9,8},{10,11... | collective-permute-start | bytes 3145736 | tf_op jit(solution)/shard_map/ppermute | solution.py:225
  69.8 11.1 %all-to-all-done.1 = bf16[32,8,1024]{2,1,0:T(8,128)(2,1)} async-done(((bf16[32,8,1024]{2,1,0:T(8,128)(2,1)}), bf16[32,8,1024]{2,1,0:T(8,128)(2,1)}, u32[]{:S(2)}, u32[]{:S(2)}) %all-to-all-start.1) | async-done | bytes 524320 | tf_op jit(solution)/shard_map/back/all_to_all | solution.py:237
  80.9 4.5 %collective-permute-start.4 = (bf16[32,8,1024]{2,1,0:T(8,128)(2,1)}, bf16[32,8,1024]{2,1,0:T(8,128)(2,1)S(1)}, u32[]{:S(2)}, u32[]{:S(2)}) collective-permute-start(bf16[32,8,1024]{2,1,0:T(8,128)(2,1)} %all-to-all-done.1), channel_id=1, source_target_pairs={{0,1},{1,0},{2,3},{3,2},{4,5},{5,4},{6,7},{7,6},{8,9},{9,8},{10,11... | collective-permute-start | bytes 1572872 | tf_op jit(solution)/shard_map/ppermute | solution.py:240
  85.4 1.4 %fusion.8 = f32[256,1024]{1,0:T(8,128)S(1)} fusion(bf16[512,2048]{1,0:T(8,128)(2,1)S(1)} %copy-done, s32[]{:T(128)S(6)} %select_n.15, bf16[256,1024]{1,0:T(8,128)(2,1)} %bitcast.4), kind=kOutput, calls=%fused_computation.13 | convolution fusion | flops 268435456 | bytes 2359300 | tf_op jit(solution)/shard_map/dot_general | solution.py:246
  86.8 0.0 collective-permute-done.3
  86.8 1.4 %fusion.5 = bf16[32,8,1024]{2,1,0:T(8,128)(2,1)S(1)} fusion(f32[256,1024]{1,0:T(8,128)S(1)} %fusion.8, bf16[512,1024]{1,0:T(8,128)(2,1)S(1)} %collective-permute-done.3, bf16[256,1024]{1,0:T(8,128)(2,1)} %bitcast.4), kind=kOutput, calls=%fused_computation.9 | convolution fusion | flops 268959744 | bytes 2883584 | tf_op jit(solution)/shard_map/dot_general | solution.py:245
  88.2 0.1 broadcast_in_dim.4
  88.3 0.3 bitcast_dynamic-update-slice_fusion.1
  88.7 0.0 copy-start.2
  88.7 0.0 collective-permute-done.4
  88.7 0.4 fusion.10
  89.1 0.5 fusion.4
  89.6 0.0 copy-done.2
  89.6 1.1 %bitcast_dynamic-update-slice_fusion = bf16[8,64,1024]{2,1,0:T(8,128)(2,1)} fusion(bf16[8,64,1024]{2,1,0:T(8,128)(2,1)} %copy-done.2, s32[]{:T(128)S(6)} %select_n.16, bf16[32,8,1024]{2,1,0:T(8,128)(2,1)S(1)} %fusion.4), kind=kLoop, calls=%fused_computation.15 | loop fusion | bytes 1048580 | tf_op jit(solution)/shard_map/dynamic_update_slice | solution.py:253
  (4 shorter events, 0.0 us)
Async XLA Ops:
  0.0 66.3 %copy-start = (bf16[512,2048]{1,0:T(8,128)(2,1)S(1)}, bf16[512,2048]{1,0:T(8,128)(2,1)}, u32[]{:S(2)}) copy-start(bf16[512,2048]{1,0:T(8,128)(2,1)} %param.8) | copy-start | bytes 6291460
  0.0 6.1 %collective-permute-start = (f32[3,3,512]{2,1,0:T(4,128)}, f32[3,3,512]{2,1,0:T(4,128)S(1)}, u32[]{:S(2)}, u32[]{:S(2)}) collective-permute-start(f32[3,3,512]{2,1,0:T(4,128)} %taps_second.3), channel_id=1, source_target_pairs={{0,1},{1,0},{2,3},{3,2},{4,5},{5,4},{6,7},{7,6},{8,9},{9,8},{10,11... | collective-permute-start | bytes 55304 | tf_op jit(solution)/shard_map/ppermute | solution.py:210
  4.5 1.4 %copy-start.3 = (s32[8]{0:T(128)S(1)}, s32[8]{0:T(128)}, u32[]{:S(2)}) copy-start(s32[8]{0:T(128)} %param.9) | copy-start | bytes 100
  6.0 43.3 %copy-start.1 = (f32[3,3,512]{2,1,0:T(4,128)S(1)}, f32[3,3,512]{2,1,0:T(4,128)}, u32[]{:S(2)}) copy-start(f32[3,3,512]{2,1,0:T(4,128)} %taps_second.3) | copy-start | bytes 55300
  6.1 43.2 %collective-permute-start.2 = (bf16[3,2048,512]{2,1,0:T(8,128)(2,1)}, bf16[3,2048,512]{2,1,0:T(8,128)(2,1)S(1)}, u32[]{:S(2)}, u32[]{:S(2)}) collective-permute-start(bf16[3,2048,512]{2,1,0:T(8,128)(2,1)} %streamed.1), channel_id=1, source_target_pairs={{0,1},{1,0},{2,3},{3,2},{4,5},{5,4},{6,7},{7,6},{8,9},{9,8},{10,11... | collective-permute-start | bytes 18874376 | tf_op jit(solution)/shard_map/ppermute | solution.py:220
  46.1 10.8 %collective-permute-start.1 = (bf16[64,2176]{1,0:T(8,128)(2,1)S(1)}, bf16[64,2176]{1,0:T(8,128)(2,1)S(1)}, u32[]{:S(2)}, u32[]{:S(2)}) collective-permute-start(bf16[64,2176]{1,0:T(8,128)(2,1)S(1)} %slice_bitcast_fusion), channel_id=1, source_target_pairs={{0,64},{64,128},{128,192},{1,65},{65,129},{129,193},{2,66},{66,130... | collective-permute-start | bytes 835592 | tf_op jit(solution)/shard_map/ppermute | solution.py:229
  61.7 19.2 %all-to-all-start.1 = ((bf16[32,8,1024]{2,1,0:T(8,128)(2,1)}), bf16[32,8,1024]{2,1,0:T(8,128)(2,1)}, u32[]{:S(2)}, u32[]{:S(2)}) async-start(bf16[32,8,1024]{2,1,0:T(8,128)(2,1)} %bitcast.3), calls=%async_computation.1 | async-start | bytes 1048576 | tf_op jit(solution)/shard_map/back/all_to_all | solution.py:237
  67.4 19.4 %collective-permute-start.3 = (bf16[512,1024]{1,0:T(8,128)(2,1)}, bf16[512,1024]{1,0:T(8,128)(2,1)S(1)}, u32[]{:S(2)}, u32[]{:S(2)}) collective-permute-start(bf16[512,1024]{1,0:T(8,128)(2,1)} %constant_dynamic-slice_fusion), channel_id=1, source_target_pairs={{0,1},{1,0},{2,3},{3,2},{4,5},{5,4},{6,7},{7,6},{8,9},{9,8},{10,11... | collective-permute-start | bytes 3145736 | tf_op jit(solution)/shard_map/ppermute | solution.py:225
  80.9 7.8 %collective-permute-start.4 = (bf16[32,8,1024]{2,1,0:T(8,128)(2,1)}, bf16[32,8,1024]{2,1,0:T(8,128)(2,1)S(1)}, u32[]{:S(2)}, u32[]{:S(2)}) collective-permute-start(bf16[32,8,1024]{2,1,0:T(8,128)(2,1)} %all-to-all-done.1), channel_id=1, source_target_pairs={{0,1},{1,0},{2,3},{3,2},{4,5},{5,4},{6,7},{7,6},{8,9},{9,8},{10,11... | collective-permute-start | bytes 1572872 | tf_op jit(solution)/shard_map/ppermute | solution.py:240
  88.7 1.0 %copy-start.2 = (bf16[8,64,1024]{2,1,0:T(8,128)(2,1)}, bf16[8,64,1024]{2,1,0:T(8,128)(2,1)S(1)}, u32[]{:S(2)}) copy-start(bf16[8,64,1024]{2,1,0:T(8,128)(2,1)S(1)} %bitcast_dynamic-update-slice_fusion.1) | copy-start | bytes 3145732

commit v4 on v3

--- a/solution.py
+++ b/solution.py
@@ -82,7 +82,18 @@
     for pad in pads:
         for kind in range(3):
             pad[kind, 0:8] = jnp.zeros((8, PAIR), jnp.float32)
+    def attention(pair):
+        conv = convs[pair % 2]
+        for head in range(PAIR // HEAD_DIM):
+            columns = slice(head * HEAD_DIM, (head + 1) * HEAD_DIM)
+            start = pair * PAIR + head * HEAD_DIM
+            out_ref[BACK:, start : start + HEAD_DIM] = attend(
+                conv[0, BACK:, columns], conv[1, :, columns], conv[2, :, columns], bias_ref[...]
+            )
+
     for pair in range(2 * per_side + 1):
+        if pair == per_side:
+            attention(pair - 1)
         if pair < 2 * per_side:
             pad, conv = pads[pair % 2], convs[pair % 2]
             for kind in range(3):
@@ -95,14 +106,8 @@
                     pad.at[kind], conv, taps[pair // per_side], mask_ref, kind,
                     (pair % per_side) * PAIR, frames,
                 )
-        if pair > 0:
-            conv = convs[(pair - 1) % 2]
-            for head in range(PAIR // HEAD_DIM):
-                columns = slice(head * HEAD_DIM, (head + 1) * HEAD_DIM)
-                start = (pair - 1) * PAIR + head * HEAD_DIM
-                out_ref[BACK:, start : start + HEAD_DIM] = attend(
-                    conv[0, BACK:, columns], conv[1, :, columns], conv[2, :, columns], bias_ref[...]
-                )
+        if pair > 0 and pair != per_side:
+            attention(pair - 1)
 
 
 def halo_kernel(x_ref, lag_ref, resident, buffer, taps_first, taps_second, first_ref, done_ref, out_ref, pad0, pad1, conv0, conv1, mask_ref, bias_ref, result, out_sem):

time: 91 us -> 90.9 us (level)
  no operation moved by 1% of the time
where the time goes in v4:
time: 90.9 us; the launch traced here: 90.6 us
  blocking collectives  39.7 us (44%)
  starting transfers between devices  18.3 us (20%)
  Pallas kernels  12.1 us (13%)
  waiting for transfers between devices  11.1 us (12%)
  local copies, waits for them, and re-layouts  4.09 us (4%)
  matrix products  3.66 us (4%)
  other arithmetic  1.44 us (2%)
    all_to_all x1, blocking collectives, shards(): rows = lax.all_to_all(packed, ('z', 'x'), 0, 0, tiled=True)  39.7 us
    all_to_all x1, waiting for transfers between devices, shards(): lax.all_to_all(attended.reshape(GROUP, frames, CORES * inner_width), ('z'...  11.1 us
    pallas_call x1, Pallas kernels, main_part(): pl.pallas_call(main_kernel, out_shape=(jax.ShapeDtypeStruct((frames, inne...  7.33 us
    pallas_call x1, Pallas kernels, halo_part(): pl.pallas_call(halo_kernel, out_shape=jax.ShapeDtypeStruct(attended.shape...  4.78 us
    all_to_all x1, starting transfers between devices, shards(): lax.all_to_all(attended.reshape(GROUP, frames, CORES * inner_width), ('z'...  4.63 us
    ppermute x1, starting transfers between devices, shards(): back_other = lax.ppermute(back, 'core', SWAP)  4.62 us
    ppermute x1, starting transfers between devices, shards(): lax.ppermute(rows[-BACK:], 'y', [(y, y + 1) for y in range(PLANES - 1)])  3.22 us
    ppermute x1, starting transfers between devices, shards(): taps_other = lax.ppermute(conv_taps, 'core', SWAP)  3.2 us
  transfers between devices with their start and end apart: 6, of which 1 were waited for; matrix products, arithmetic and copies ran while one was open for 8% of the time, Pallas kernels for 8%

profile of v4, /device:TPU:1, one launch (start us, length us, event | category | flops | bytes accessed | tf_op | source)
XLA Modules:
  0.0 90.6 jit_solution(5744510447179233740)
XLA Ops:
  0.0 0.0 copy-start
  0.0 3.2 %collective-permute-start = (f32[3,3,512]{2,1,0:T(4,128)}, f32[3,3,512]{2,1,0:T(4,128)S(1)}, u32[]{:S(2)}, u32[]{:S(2)}) collective-permute-start(f32[3,3,512]{2,1,0:T(4,128)} %taps_second.3), channel_id=1, source_target_pairs={{0,1},{1,0},{2,3},{3,2},{4,5},{5,4},{6,7},{7,6},{8,9},{9,8},{10,11... | collective-permute-start | bytes 55304 | tf_op jit(solution)/shard_map/ppermute | solution.py:215
  3.2 1.3 %constant_dynamic-slice_fusion.1 = bf16[8,32,2048]{2,1,0:T(8,128)(2,1)S(1)} fusion(bf16[8,64,2048]{2,1,0:T(8,128)(2,1)} %param.5, s32[]{:T(128)S(6)} %select_n.13), kind=kLoop, calls=%fused_computation.27 | loop fusion | bytes 2097156 | tf_op jit(solution)/shard_map/dynamic_slice | solution.py:216
  4.5 0.0 copy-start.3
  4.5 0.7 fusion
  5.3 0.6 fusion.6
  5.9 0.0 copy-done.3
  5.9 0.1 broadcast_in_dim.5
  6.0 0.0 copy-start.1
  6.0 0.1 pad_maximum_fusion
  6.1 0.0 collective-permute-done.taps_first
  6.1 0.2 collective-permute-start.2
  6.3 39.7 %all_to_all.10 = bf16[32,8,2176]{2,1,0:T(8,128)(2,1)S(1)} all-to-all(bf16[32,8,2176]{2,1,0:T(8,128)(2,1)S(1)} %pad_maximum_fusion), channel_id=1, replica_groups=mesh['y'=4,'z'=8,'x'=4,'core'=2] {'z','x'}, dimensions={0} | all-to-all | bytes 2228224 | tf_op jit(solution)/shard_map/gather/all_to_all | solution.py:227
  46.1 3.2 %collective-permute-start.1 = (bf16[64,2176]{1,0:T(8,128)(2,1)S(1)}, bf16[64,2176]{1,0:T(8,128)(2,1)S(1)}, u32[]{:S(2)}, u32[]{:S(2)}) collective-permute-start(bf16[64,2176]{1,0:T(8,128)(2,1)S(1)} %slice_bitcast_fusion), channel_id=1, source_target_pairs={{0,64},{64,128},{128,192},{1,65},{65,129},{129,193},{2,66},{66,130... | collective-permute-start | bytes 835592 | tf_op jit(solution)/shard_map/ppermute | solution.py:234
  49.3 0.0 collective-permute-done.2.resident
  49.3 0.0 copy-done.1
  49.3 7.3 %main_rows.1 = (bf16[256,1024]{1,0:T(8,128)(2,1)}, f32[3,64,1024]{2,1,0:T(8,128)S(1)}, bf16[3,2048,512]{2,1,0:T(8,128)(2,1)S(1)}) custom-call(bf16[256,2176]{1,0:T(8,128)(2,1)S(1)} %bitcast.19, bf16[3,2048,512]{2,1,0:T(8,128)(2,1)S(1)} %collective-permute-done.2.resident, bf16[3,2048,512]{2,1,0:T(8,128)(2,1)} %streamed.1, ...), custom_call_target="tpu_custom_call" | custom-call | tf_op jit(solution)/shard_map/main_rows/pallas_call | solution.py:172
  56.7 0.0 collective-permute-done.1.x_ref
  56.7 4.8 %halo_rows.1 = bf16[256,1024]{1,0:T(8,128)(2,1)} custom-call(bf16[64,2176]{1,0:T(8,128)(2,1)S(1)} %collective-permute-done.1.x_ref, bf16[64,128]{1,0:T(8,128)(2,1)S(1)} %slice.29.lag_ref, bf16[3,2048,512]{2,1,0:T(8,128)(2,1)S(1)} %collective-permute-done.2.resident, ...), custom_call_target="tpu_custom_call", output_to_operand_aliasing={{}: (7, {})} | custom-call | tf_op jit(solution)/shard_map/halo_rows/pallas_call | solution.py:191
  61.5 4.6 %all-to-all-start.1 = ((bf16[32,8,1024]{2,1,0:T(8,128)(2,1)}), bf16[32,8,1024]{2,1,0:T(8,128)(2,1)}, u32[]{:S(2)}, u32[]{:S(2)}) async-start(bf16[32,8,1024]{2,1,0:T(8,128)(2,1)} %bitcast.3), calls=%async_computation.1 | async-start | bytes 1048576 | tf_op jit(solution)/shard_map/back/all_to_all | solution.py:242
  66.1 0.0 copy-done
  66.1 1.1 %constant_dynamic-slice_fusion = bf16[512,1024]{1,0:T(8,128)(2,1)} fusion(bf16[512,2048]{1,0:T(8,128)(2,1)S(1)} %copy-done, s32[]{:T(128)S(6)} %select_n.14), kind=kLoop, calls=%fused_computation.26 | loop fusion | bytes 2097156 | tf_op jit(solution)/shard_map/theirs/dynamic_slice | solution.py:229
  67.2 2.4 %collective-permute-start.3 = (bf16[512,1024]{1,0:T(8,128)(2,1)}, bf16[512,1024]{1,0:T(8,128)(2,1)S(1)}, u32[]{:S(2)}, u32[]{:S(2)}) collective-permute-start(bf16[512,1024]{1,0:T(8,128)(2,1)} %constant_dynamic-slice_fusion), channel_id=1, source_target_pairs={{0,1},{1,0},{2,3},{3,2},{4,5},{5,4},{6,7},{7,6},{8,9},{9,8},{10,11... | collective-permute-start | bytes 3145736 | tf_op jit(solution)/shard_map/ppermute | solution.py:230
  69.6 11.1 %all-to-all-done.1 = bf16[32,8,1024]{2,1,0:T(8,128)(2,1)} async-done(((bf16[32,8,1024]{2,1,0:T(8,128)(2,1)}), bf16[32,8,1024]{2,1,0:T(8,128)(2,1)}, u32[]{:S(2)}, u32[]{:S(2)}) %all-to-all-start.1) | async-done | bytes 524320 | tf_op jit(solution)/shard_map/back/all_to_all | solution.py:242
  80.7 4.6 %collective-permute-start.4 = (bf16[32,8,1024]{2,1,0:T(8,128)(2,1)}, bf16[32,8,1024]{2,1,0:T(8,128)(2,1)S(1)}, u32[]{:S(2)}, u32[]{:S(2)}) collective-permute-start(bf16[32,8,1024]{2,1,0:T(8,128)(2,1)} %all-to-all-done.1), channel_id=1, source_target_pairs={{0,1},{1,0},{2,3},{3,2},{4,5},{5,4},{6,7},{7,6},{8,9},{9,8},{10,11... | collective-permute-start | bytes 1572872 | tf_op jit(solution)/shard_map/ppermute | solution.py:245
  85.3 1.4 %fusion.8 = f32[256,1024]{1,0:T(8,128)S(1)} fusion(bf16[512,2048]{1,0:T(8,128)(2,1)S(1)} %copy-done, s32[]{:T(128)S(6)} %select_n.15, bf16[256,1024]{1,0:T(8,128)(2,1)} %bitcast.4), kind=kOutput, calls=%fused_computation.13 | convolution fusion | flops 268435456 | bytes 2359300 | tf_op jit(solution)/shard_map/dot_general | solution.py:251
  86.7 0.0 collective-permute-done.3
  86.7 1.4 %fusion.5 = bf16[32,8,1024]{2,1,0:T(8,128)(2,1)S(1)} fusion(f32[256,1024]{1,0:T(8,128)S(1)} %fusion.8, bf16[512,1024]{1,0:T(8,128)(2,1)S(1)} %collective-permute-done.3, bf16[256,1024]{1,0:T(8,128)(2,1)} %bitcast.4), kind=kOutput, calls=%fused_computation.9 | convolution fusion | flops 268959744 | bytes 2883584 | tf_op jit(solution)/shard_map/dot_general | solution.py:250
  88.1 0.1 broadcast_in_dim.4
  88.2 0.3 bitcast_dynamic-update-slice_fusion.1
  88.5 0.0 copy-start.2
  88.5 0.0 collective-permute-done.4
  88.6 0.4 fusion.10
  89.0 0.5 fusion.4
  89.5 0.0 copy-done.2
  89.5 1.1 %bitcast_dynamic-update-slice_fusion = bf16[8,64,1024]{2,1,0:T(8,128)(2,1)} fusion(bf16[8,64,1024]{2,1,0:T(8,128)(2,1)} %copy-done.2, s32[]{:T(128)S(6)} %select_n.16, bf16[32,8,1024]{2,1,0:T(8,128)(2,1)S(1)} %fusion.4), kind=kLoop, calls=%fused_computation.15 | loop fusion | bytes 1048580 | tf_op jit(solution)/shard_map/dynamic_update_slice | solution.py:258
  (4 shorter events, 0.0 us)
Async XLA Ops:
  0.0 66.1 %copy-start = (bf16[512,2048]{1,0:T(8,128)(2,1)S(1)}, bf16[512,2048]{1,0:T(8,128)(2,1)}, u32[]{:S(2)}) copy-start(bf16[512,2048]{1,0:T(8,128)(2,1)} %param.8) | copy-start | bytes 6291460
  0.0 6.1 %collective-permute-start = (f32[3,3,512]{2,1,0:T(4,128)}, f32[3,3,512]{2,1,0:T(4,128)S(1)}, u32[]{:S(2)}, u32[]{:S(2)}) collective-permute-start(f32[3,3,512]{2,1,0:T(4,128)} %taps_second.3), channel_id=1, source_target_pairs={{0,1},{1,0},{2,3},{3,2},{4,5},{5,4},{6,7},{7,6},{8,9},{9,8},{10,11... | collective-permute-start | bytes 55304 | tf_op jit(solution)/shard_map/ppermute | solution.py:215
  4.5 1.4 %copy-start.3 = (s32[8]{0:T(128)S(1)}, s32[8]{0:T(128)}, u32[]{:S(2)}) copy-start(s32[8]{0:T(128)} %param.9) | copy-start | bytes 100
  6.0 43.3 %copy-start.1 = (f32[3,3,512]{2,1,0:T(4,128)S(1)}, f32[3,3,512]{2,1,0:T(4,128)}, u32[]{:S(2)}) copy-start(f32[3,3,512]{2,1,0:T(4,128)} %taps_second.3) | copy-start | bytes 55300
  6.1 43.2 %collective-permute-start.2 = (bf16[3,2048,512]{2,1,0:T(8,128)(2,1)}, bf16[3,2048,512]{2,1,0:T(8,128)(2,1)S(1)}, u32[]{:S(2)}, u32[]{:S(2)}) collective-permute-start(bf16[3,2048,512]{2,1,0:T(8,128)(2,1)} %streamed.1), channel_id=1, source_target_pairs={{0,1},{1,0},{2,3},{3,2},{4,5},{5,4},{6,7},{7,6},{8,9},{9,8},{10,11... | collective-permute-start | bytes 18874376 | tf_op jit(solution)/shard_map/ppermute | solution.py:225
  46.1 10.6 %collective-permute-start.1 = (bf16[64,2176]{1,0:T(8,128)(2,1)S(1)}, bf16[64,2176]{1,0:T(8,128)(2,1)S(1)}, u32[]{:S(2)}, u32[]{:S(2)}) collective-permute-start(bf16[64,2176]{1,0:T(8,128)(2,1)S(1)} %slice_bitcast_fusion), channel_id=1, source_target_pairs={{0,64},{64,128},{128,192},{1,65},{65,129},{129,193},{2,66},{66,130... | collective-permute-start | bytes 835592 | tf_op jit(solution)/shard_map/ppermute | solution.py:234
  61.5 19.2 %all-to-all-start.1 = ((bf16[32,8,1024]{2,1,0:T(8,128)(2,1)}), bf16[32,8,1024]{2,1,0:T(8,128)(2,1)}, u32[]{:S(2)}, u32[]{:S(2)}) async-start(bf16[32,8,1024]{2,1,0:T(8,128)(2,1)} %bitcast.3), calls=%async_computation.1 | async-start | bytes 1048576 | tf_op jit(solution)/shard_map/back/all_to_all | solution.py:242
  67.2 19.5 %collective-permute-start.3 = (bf16[512,1024]{1,0:T(8,128)(2,1)}, bf16[512,1024]{1,0:T(8,128)(2,1)S(1)}, u32[]{:S(2)}, u32[]{:S(2)}) collective-permute-start(bf16[512,1024]{1,0:T(8,128)(2,1)} %constant_dynamic-slice_fusion), channel_id=1, source_target_pairs={{0,1},{1,0},{2,3},{3,2},{4,5},{5,4},{6,7},{7,6},{8,9},{9,8},{10,11... | collective-permute-start | bytes 3145736 | tf_op jit(solution)/shard_map/ppermute | solution.py:230
  80.7 7.9 %collective-permute-start.4 = (bf16[32,8,1024]{2,1,0:T(8,128)(2,1)}, bf16[32,8,1024]{2,1,0:T(8,128)(2,1)S(1)}, u32[]{:S(2)}, u32[]{:S(2)}) collective-permute-start(bf16[32,8,1024]{2,1,0:T(8,128)(2,1)} %all-to-all-done.1), channel_id=1, source_target_pairs={{0,1},{1,0},{2,3},{3,2},{4,5},{5,4},{6,7},{7,6},{8,9},{9,8},{10,11... | collective-permute-start | bytes 1572872 | tf_op jit(solution)/shard_map/ppermute | solution.py:245
  88.5 1.0 %copy-start.2 = (bf16[8,64,1024]{2,1,0:T(8,128)(2,1)}, bf16[8,64,1024]{2,1,0:T(8,128)(2,1)S(1)}, u32[]{:S(2)}) copy-start(bf16[8,64,1024]{2,1,0:T(8,128)(2,1)S(1)} %bitcast_dynamic-update-slice_fusion.1) | copy-start | bytes 3145732
